TPU v7x, 512 devices: a whole 4x8x8 slice. The times are simulated.
512 devices in a mesh: kq: 128 (over y, z, core), band: 4 (over x).
Axes of the slice: x: 4, y: 8, z: 8, core: 2. Of those that a mesh axis runs over, the one named last changes fastest.
Arguments:
- band_functions: bfloat16 [128, 2, 16, 4096], P('kq', None, 'band'), may hold values from -6 to 6
- screening: bfloat16 [128, 2, 512, 512], P('kq'), may hold values from -0.1875 to 0.1875
- exciton: bfloat16 [128, 2, 64], P('kq'), may hold values from -6 to 6
- pair_list: int32 [1024, 2], P('kq'), may hold values from 0 to 127, as said below
Outputs:
- kernel_action: float32 [128, 2, 64], P('kq', None, 'band')
Inputs may be any that keep to these rules, and one draw needn't show every extreme that they name: `pair_list`: rows d * 8 to d * 8 + 7 are the pairs of momentum transfer d: their second point is (first point - d) mod 128. Row d * 8 + s has second point c_s, the same for every d, and first point (d + c_s) mod 128; the c_s are distinct. Every k-point is the first point of exactly 8 pairs.
All inputs are finite; a program needn't handle non-finite values.
Results may differ from a plain program's by a relative error of at most 0.0074.
Values may be sent and summed in bfloat16 or wider, within the bound.
No kernel may reach another device: no remote copies, remote signals or barrier semaphores. Data moves between devices by JAX's collectives and lax.ppermute only.
A program may use at most 64 MiB of HBM per device.

v0:
```python
import math

import jax
import jax.numpy as jnp
from jax import lax
from jax.sharding import PartitionSpec as P

NV = 8
NC = 8
GRID_SIDE = 16
GSIDE = 8


def phase_tables(first_cell, cell_count, grid_side, plane_side, planes):
    grid_cells = first_cell + jnp.arange(cell_count, dtype=jnp.int32)
    cell_x = grid_cells // (grid_side * grid_side)
    cell_y = grid_cells // grid_side % grid_side
    cell_z = grid_cells % grid_side
    wave_index = jnp.arange(planes, dtype=jnp.int32)
    half_side = plane_side // 2
    wave_x = wave_index // (plane_side * plane_side) - half_side
    wave_y = wave_index // plane_side % plane_side - half_side
    wave_z = wave_index % plane_side - half_side
    phase_index = (
        cell_x[:, None] * wave_x[None, :]
        + cell_y[:, None] * wave_y[None, :]
        + cell_z[:, None] * wave_z[None, :]
    ) % grid_side
    angles = phase_index.astype(jnp.float32) * (2.0 * math.pi / grid_side)
    return (jnp.cos(angles).astype(jnp.bfloat16), jnp.sin(angles).astype(jnp.bfloat16))


def pair_densities(left_funcs, right_funcs):
    left_re = left_funcs[:, 0, :, None, :].astype(jnp.float32)
    left_im = left_funcs[:, 1, :, None, :].astype(jnp.float32)
    right_re = right_funcs[:, 0, None, :, :].astype(jnp.float32)
    right_im = right_funcs[:, 1, None, :, :].astype(jnp.float32)
    dens_re = left_re * right_re + left_im * right_im
    dens_im = left_re * right_im - left_im * right_re
    grid_total = left_funcs.shape[-1]
    return (
        dens_re.astype(jnp.bfloat16).reshape(left_funcs.shape[0], -1, grid_total),
        dens_im.astype(jnp.bfloat16).reshape(left_funcs.shape[0], -1, grid_total),
    )


def to_waves(dens_re, dens_im, planes):
    row_count = dens_re.shape[0]
    grid_total = dens_re.shape[1]
    block_size = min(512, grid_total)
    stacked = jnp.concatenate([dens_re, dens_im], axis=0)

    def add_block(block_index, totals):
        first_cell = block_index * block_size
        cos_table, sin_table = phase_tables(first_cell, block_size, GRID_SIDE, GSIDE, planes)
        piece = lax.dynamic_slice_in_dim(stacked, first_cell, block_size, 1)
        with_cos = totals[0] + jnp.dot(piece, cos_table, preferred_element_type=jnp.float32)
        with_sin = totals[1] + jnp.dot(piece, sin_table, preferred_element_type=jnp.float32)
        return (with_cos, with_sin)

    empty = jnp.zeros((2 * row_count, planes), jnp.float32)
    with_cos, with_sin = lax.fori_loop(0, grid_total // block_size, add_block, (empty, empty))
    scale = 1.0 / math.sqrt(grid_total)
    wave_re = (with_cos[:row_count] + with_sin[row_count:]) * scale
    wave_im = (with_cos[row_count:] - with_sin[:row_count]) * scale
    return (wave_re.astype(jnp.bfloat16), wave_im.astype(jnp.bfloat16))


def split_blocks(funcs, band_count, val_block):
    shaped = funcs.reshape(funcs.shape[0], 2, band_count, 2, val_block, funcs.shape[-1])
    valence = shaped[:, :, :, 0].reshape(funcs.shape[0], 2, band_count * val_block, funcs.shape[-1])
    conduction = shaped[:, :, :, 1].reshape(
        funcs.shape[0], 2, band_count * val_block, funcs.shape[-1]
    )
    return (valence, conduction)


def local(band_functions, screening, exciton, pair_list):
    pairs_here = pair_list.shape[0]
    band_count = lax.axis_size("band")
    band_place = lax.axis_index("band")
    val_block = NV // band_count
    grid_total = band_functions.shape[-1]
    planes = screening.shape[-1]
    point_count = band_functions.shape[0] * lax.axis_size("kq")
    amp_width = exciton.shape[2]
    ends = jnp.concatenate([pair_list[:, 0], pair_list[:, 1]])
    end_count = ends.shape[0]
    func_piece = lax.all_gather(band_functions, "kq", axis=0, tiled=True)
    amp_piece = lax.all_gather(exciton, "kq", axis=0, tiled=True)
    piece_rows = func_piece.shape[0]
    picker = (ends[:, None] == jnp.arange(piece_rows, dtype=jnp.int32)[None, :]).astype(
        jnp.bfloat16
    )
    picked_funcs = jnp.dot(
        picker, func_piece.reshape(piece_rows, -1), preferred_element_type=jnp.float32
    )
    picked_amps = jnp.dot(
        picker, amp_piece.reshape(piece_rows, -1), preferred_element_type=jnp.float32
    )
    chosen_funcs = picked_funcs.astype(jnp.bfloat16)
    chosen_amps = picked_amps.astype(jnp.bfloat16)
    chosen_funcs = chosen_funcs.reshape(end_count, 2, 2 * val_block, grid_total)
    first_funcs = chosen_funcs[:pairs_here]
    second_funcs = chosen_funcs[pairs_here:]
    first_amps = chosen_amps[:pairs_here].reshape(pairs_here, 2, amp_width).astype(jnp.float32)
    second_amps = chosen_amps[pairs_here:].reshape(pairs_here, 2, amp_width).astype(jnp.float32)
    own_valence = first_funcs[:, :, :val_block]
    second_whole = lax.all_gather(second_funcs, "band", axis=2, tiled=True)
    second_valence, second_conduction = split_blocks(second_whole, band_count, val_block)
    left_conduction = first_funcs[:, :, val_block:]
    val_re, val_im = pair_densities(own_valence, second_valence)
    cond_re, cond_im = pair_densities(left_conduction, second_conduction)
    val_rows = val_re.shape[1]
    all_re = jnp.concatenate([val_re, cond_re], axis=1).reshape(-1, grid_total)
    all_im = jnp.concatenate([val_im, cond_im], axis=1).reshape(-1, grid_total)
    wave_re, wave_im = to_waves(all_re, all_im, planes)
    wave_re = wave_re.reshape(pairs_here, -1, planes)
    wave_im = wave_im.reshape(pairs_here, -1, planes)
    wv_re = wave_re[:, :val_rows].reshape(-1, planes)
    wv_im = wave_im[:, :val_rows].reshape(-1, planes)
    cond_waves = jnp.stack([wave_re[:, val_rows:], wave_im[:, val_rows:]], axis=1)
    cond_waves = lax.all_gather(cond_waves, "band", axis=2, tiled=True)
    contract = (((1,), (1,)), ((), ()))
    weight_re = screening[0, 0]
    weight_im = screening[0, 1]
    val_stack = jnp.concatenate([wv_re, wv_im], axis=0)
    with_real = lax.dot_general(val_stack, weight_re, contract, preferred_element_type=jnp.float32)
    with_imag = lax.dot_general(val_stack, weight_im, contract, preferred_element_type=jnp.float32)
    half_rows = wv_re.shape[0]
    scr_re = (
        (with_real[:half_rows] - with_imag[half_rows:])
        .astype(jnp.bfloat16)
        .reshape(pairs_here, -1, planes)
    )
    scr_im = (
        (with_real[half_rows:] + with_imag[:half_rows])
        .astype(jnp.bfloat16)
        .reshape(pairs_here, -1, planes)
    )
    cond_wave_re = cond_waves[:, 0]
    cond_wave_im = cond_waves[:, 1]

    def batched(left_side, right_side):
        return jnp.einsum("pag,pbg->pab", left_side, right_side, preferred_element_type=jnp.float32)

    kern_re = (batched(cond_wave_re, scr_re) + batched(cond_wave_im, scr_im)) / planes
    kern_im = (batched(cond_wave_re, scr_im) - batched(cond_wave_im, scr_re)) / planes
    kern_re = jnp.transpose(
        kern_re.reshape(pairs_here, NC, NC, val_block, NV), (0, 3, 1, 4, 2)
    ).reshape(pairs_here, val_block * NC, NV * NC)
    kern_im = jnp.transpose(
        kern_im.reshape(pairs_here, NC, NC, val_block, NV), (0, 3, 1, 4, 2)
    ).reshape(pairs_here, val_block * NC, NV * NC)
    highest = lax.Precision.HIGHEST
    direct_re = jnp.einsum(
        "pab,pb->pa", kern_re, second_amps[:, 0], precision=highest
    ) - jnp.einsum("pab,pb->pa", kern_im, second_amps[:, 1], precision=highest)
    direct_im = jnp.einsum(
        "pab,pb->pa", kern_re, second_amps[:, 1], precision=highest
    ) + jnp.einsum("pab,pb->pa", kern_im, second_amps[:, 0], precision=highest)
    row_offset = band_place * (val_block * NC)
    own_amps = lax.dynamic_slice_in_dim(first_amps, row_offset, val_block * NC, 2)
    back_re = jnp.einsum("pab,pa->pb", kern_re, own_amps[:, 0], precision=highest) + jnp.einsum(
        "pab,pa->pb", kern_im, own_amps[:, 1], precision=highest
    )
    back_im = jnp.einsum("pab,pa->pb", kern_re, own_amps[:, 1], precision=highest) - jnp.einsum(
        "pab,pa->pb", kern_im, own_amps[:, 0], precision=highest
    )
    direct_part = jnp.stack([direct_re, direct_im], axis=1)
    direct_full = lax.dynamic_update_slice_in_dim(
        jnp.zeros((pairs_here, 2, amp_width), jnp.float32), direct_part, row_offset, 2
    )
    back_full = jnp.stack([back_re, back_im], axis=1)
    point_ids = jnp.arange(point_count, dtype=jnp.int32)
    first_onehot = (pair_list[:, 0][:, None] == point_ids[None, :]).astype(jnp.float32)
    second_onehot = (pair_list[:, 1][:, None] == point_ids[None, :]).astype(jnp.float32)
    terms = jnp.einsum("pk,pcj->kcj", first_onehot, direct_full, precision=highest) + jnp.einsum(
        "pk,pcj->kcj", second_onehot, back_full, precision=highest
    )
    widened = lax.psum_scatter(terms, "kq", scatter_dimension=0, tiled=True)
    result = lax.psum_scatter(widened, "band", scatter_dimension=2, tiled=True)
    return result


def solution(mesh):
    return jax.shard_map(
        local,
        mesh=mesh,
        in_specs=(
            P("kq", None, "band", None),
            P("kq", None, None, None),
            P("kq", None, None),
            P("kq", None),
        ),
        out_specs=P("kq", None, "band"),
        check_vma=False,
    )
```

profile of v0, /device:TPU:1, one launch (start us, length us, event | category | flops | bytes accessed | tf_op | source)
XLA Modules:
  0.0 517.2 jit_solution(2458616163616027740)
XLA Ops:
  8.1 96.0 %all-gather.4.cloned.1.call-done = bf16[128,2,4,4096]{3,2,1,0:T(4,128)(2,1)} async-done(((bf16[1,2,4,4096]{3,2,1,0:T(4,128)(2,1)}), bf16[128,2,4,4096]{3,2,1,0:T(4,128)(2,1)}) %all-gather.4.cloned.1.call-update) | async-done | bytes 8388624 | tf_op jit(solution)/shard_map/all_gather | solution.py:89
  104.2 14.5 %reshape.216 = bf16[128,32768]{1,0:T(8,128)(2,1)} reshape(bf16[128,2,4,4096]{3,2,1,0:T(4,128)(2,1)} %all-gather.4.cloned.1.call-done) | data formatting | bytes 16777216 | tf_op jit(solution)/shard_map/reshape | solution.py:96
  118.6 4.6 convolution_convert_fusion
  123.3 0.9 fusion.86
  124.3 43.5 %all_gather.15 = bf16[128,2,64]{2,1,0:T(2,128)(2,1)S(1)} all-gather(bf16[1,2,64]{2,1,0:T(2,128)(2,1)S(1)} %copy-done.1), channel_id=1, replica_groups=mesh['kq'=128,'band'=4] {'kq'}, dimensions={0}, use_global_device_ids=true | all-gather | bytes 33024 | tf_op jit(solution)/shard_map/all_gather | solution.py:90
  169.0 1.7 fusion.85
  175.0 2.5 pad_maximum_fusion
  177.4 92.7 %while.19 = (s32[]{:T(128)}, f32[512,512]{1,0:T(8,128)S(1)}, f32[512,512]{1,0:T(8,128)S(1)}, bf16[512,4096]{1,0:T(8,128)(2,1)}, s32[]{:T(128)}, /*index=5*/s32[]{:T(128)}, s32[]{:T(128)}, s32[]{:T(128)}) while((s32[]{:T(128)}, f32[512,512]{1,0:T(8,128)S(1)}, f32[512,512]{1,0:T(8,128)S(1)}, bf16[512,4096]{1,0:T(8,128)(2,1)}, ...), condition=%wide.region_1.2_spmd.clone, body=%wide.region_0.1_spmd.clone.sunk | while | flops 547922432 | bytes 5279902 | solution.py:62
  177.5 5.8 %convolution_add_fusion.7 = f32[512,512]{1,0:T(8,128)S(1)} fusion(f32[512,512]{1,0:T(8,128)S(1)} %get-tuple-element.275, s32[512]{0:T(512)S(1)} %get-tuple-element.259, s32[512]{0:T(512)S(1)} %get-tuple-element.260, s32[512]{0:T(512)S(1)} %get-tuple-element.261, s32[512]{0:T(512)S(1)} %get-tuple-element.262, s32[512]{0:T(512)S(1)} %get-tuple-element.263, ...), kind=kOutput, calls=%fused_computation.3.clone.1 | convolution fusion | flops 273940480 | bytes 2633733 | tf_op jit(solution)/shard_map/while/body/eval_jaxpr/dot_general | solution.py:58
  183.3 5.7 %convolution_add_fusion.6 = f32[512,512]{1,0:T(8,128)S(1)} fusion(f32[512,512]{1,0:T(8,128)S(1)} %get-tuple-element.274, s32[512]{0:T(512)S(1)} %get-tuple-element.259, s32[512]{0:T(512)S(1)} %get-tuple-element.260, s32[512]{0:T(512)S(1)} %get-tuple-element.261, s32[512]{0:T(512)S(1)} %get-tuple-element.262, s32[512]{0:T(512)S(1)} %get-tuple-element.263, ...), kind=kOutput, calls=%fused_computation.4.clone.1 | convolution fusion | flops 273940480 | bytes 2633733 | tf_op jit(solution)/shard_map/while/body/eval_jaxpr/dot_general | solution.py:57
  189.1 5.8 %convolution_add_fusion.7 = f32[512,512]{1,0:T(8,128)S(1)} fusion(f32[512,512]{1,0:T(8,128)S(1)} %get-tuple-element.275, s32[512]{0:T(512)S(1)} %get-tuple-element.259, s32[512]{0:T(512)S(1)} %get-tuple-element.260, s32[512]{0:T(512)S(1)} %get-tuple-element.261, s32[512]{0:T(512)S(1)} %get-tuple-element.262, s32[512]{0:T(512)S(1)} %get-tuple-element.263, ...), kind=kOutput, calls=%fused_computation.3.clone.1 | convolution fusion | flops 273940480 | bytes 2633733 | tf_op jit(solution)/shard_map/while/body/eval_jaxpr/dot_general | solution.py:58
  194.9 5.7 %convolution_add_fusion.6 = f32[512,512]{1,0:T(8,128)S(1)} fusion(f32[512,512]{1,0:T(8,128)S(1)} %get-tuple-element.274, s32[512]{0:T(512)S(1)} %get-tuple-element.259, s32[512]{0:T(512)S(1)} %get-tuple-element.260, s32[512]{0:T(512)S(1)} %get-tuple-element.261, s32[512]{0:T(512)S(1)} %get-tuple-element.262, s32[512]{0:T(512)S(1)} %get-tuple-element.263, ...), kind=kOutput, calls=%fused_computation.4.clone.1 | convolution fusion | flops 273940480 | bytes 2633733 | tf_op jit(solution)/shard_map/while/body/eval_jaxpr/dot_general | solution.py:57
  200.7 5.8 %convolution_add_fusion.7 = f32[512,512]{1,0:T(8,128)S(1)} fusion(f32[512,512]{1,0:T(8,128)S(1)} %get-tuple-element.275, s32[512]{0:T(512)S(1)} %get-tuple-element.259, s32[512]{0:T(512)S(1)} %get-tuple-element.260, s32[512]{0:T(512)S(1)} %get-tuple-element.261, s32[512]{0:T(512)S(1)} %get-tuple-element.262, s32[512]{0:T(512)S(1)} %get-tuple-element.263, ...), kind=kOutput, calls=%fused_computation.3.clone.1 | convolution fusion | flops 273940480 | bytes 2633733 | tf_op jit(solution)/shard_map/while/body/eval_jaxpr/dot_general | solution.py:58
  206.4 5.7 %convolution_add_fusion.6 = f32[512,512]{1,0:T(8,128)S(1)} fusion(f32[512,512]{1,0:T(8,128)S(1)} %get-tuple-element.274, s32[512]{0:T(512)S(1)} %get-tuple-element.259, s32[512]{0:T(512)S(1)} %get-tuple-element.260, s32[512]{0:T(512)S(1)} %get-tuple-element.261, s32[512]{0:T(512)S(1)} %get-tuple-element.262, s32[512]{0:T(512)S(1)} %get-tuple-element.263, ...), kind=kOutput, calls=%fused_computation.4.clone.1 | convolution fusion | flops 273940480 | bytes 2633733 | tf_op jit(solution)/shard_map/while/body/eval_jaxpr/dot_general | solution.py:57
  212.3 5.8 %convolution_add_fusion.7 = f32[512,512]{1,0:T(8,128)S(1)} fusion(f32[512,512]{1,0:T(8,128)S(1)} %get-tuple-element.275, s32[512]{0:T(512)S(1)} %get-tuple-element.259, s32[512]{0:T(512)S(1)} %get-tuple-element.260, s32[512]{0:T(512)S(1)} %get-tuple-element.261, s32[512]{0:T(512)S(1)} %get-tuple-element.262, s32[512]{0:T(512)S(1)} %get-tuple-element.263, ...), kind=kOutput, calls=%fused_computation.3.clone.1 | convolution fusion | flops 273940480 | bytes 2633733 | tf_op jit(solution)/shard_map/while/body/eval_jaxpr/dot_general | solution.py:58
  218.0 5.7 %convolution_add_fusion.6 = f32[512,512]{1,0:T(8,128)S(1)} fusion(f32[512,512]{1,0:T(8,128)S(1)} %get-tuple-element.274, s32[512]{0:T(512)S(1)} %get-tuple-element.259, s32[512]{0:T(512)S(1)} %get-tuple-element.260, s32[512]{0:T(512)S(1)} %get-tuple-element.261, s32[512]{0:T(512)S(1)} %get-tuple-element.262, s32[512]{0:T(512)S(1)} %get-tuple-element.263, ...), kind=kOutput, calls=%fused_computation.4.clone.1 | convolution fusion | flops 273940480 | bytes 2633733 | tf_op jit(solution)/shard_map/while/body/eval_jaxpr/dot_general | solution.py:57
  223.9 5.8 %convolution_add_fusion.7 = f32[512,512]{1,0:T(8,128)S(1)} fusion(f32[512,512]{1,0:T(8,128)S(1)} %get-tuple-element.275, s32[512]{0:T(512)S(1)} %get-tuple-element.259, s32[512]{0:T(512)S(1)} %get-tuple-element.260, s32[512]{0:T(512)S(1)} %get-tuple-element.261, s32[512]{0:T(512)S(1)} %get-tuple-element.262, s32[512]{0:T(512)S(1)} %get-tuple-element.263, ...), kind=kOutput, calls=%fused_computation.3.clone.1 | convolution fusion | flops 273940480 | bytes 2633733 | tf_op jit(solution)/shard_map/while/body/eval_jaxpr/dot_general | solution.py:58
  229.6 5.7 %convolution_add_fusion.6 = f32[512,512]{1,0:T(8,128)S(1)} fusion(f32[512,512]{1,0:T(8,128)S(1)} %get-tuple-element.274, s32[512]{0:T(512)S(1)} %get-tuple-element.259, s32[512]{0:T(512)S(1)} %get-tuple-element.260, s32[512]{0:T(512)S(1)} %get-tuple-element.261, s32[512]{0:T(512)S(1)} %get-tuple-element.262, s32[512]{0:T(512)S(1)} %get-tuple-element.263, ...), kind=kOutput, calls=%fused_computation.4.clone.1 | convolution fusion | flops 273940480 | bytes 2633733 | tf_op jit(solution)/shard_map/while/body/eval_jaxpr/dot_general | solution.py:57
  235.5 5.8 %convolution_add_fusion.7 = f32[512,512]{1,0:T(8,128)S(1)} fusion(f32[512,512]{1,0:T(8,128)S(1)} %get-tuple-element.275, s32[512]{0:T(512)S(1)} %get-tuple-element.259, s32[512]{0:T(512)S(1)} %get-tuple-element.260, s32[512]{0:T(512)S(1)} %get-tuple-element.261, s32[512]{0:T(512)S(1)} %get-tuple-element.262, s32[512]{0:T(512)S(1)} %get-tuple-element.263, ...), kind=kOutput, calls=%fused_computation.3.clone.1 | convolution fusion | flops 273940480 | bytes 2633733 | tf_op jit(solution)/shard_map/while/body/eval_jaxpr/dot_general | solution.py:58
  241.2 5.7 %convolution_add_fusion.6 = f32[512,512]{1,0:T(8,128)S(1)} fusion(f32[512,512]{1,0:T(8,128)S(1)} %get-tuple-element.274, s32[512]{0:T(512)S(1)} %get-tuple-element.259, s32[512]{0:T(512)S(1)} %get-tuple-element.260, s32[512]{0:T(512)S(1)} %get-tuple-element.261, s32[512]{0:T(512)S(1)} %get-tuple-element.262, s32[512]{0:T(512)S(1)} %get-tuple-element.263, ...), kind=kOutput, calls=%fused_computation.4.clone.1 | convolution fusion | flops 273940480 | bytes 2633733 | tf_op jit(solution)/shard_map/while/body/eval_jaxpr/dot_general | solution.py:57
  247.1 5.8 %convolution_add_fusion.7 = f32[512,512]{1,0:T(8,128)S(1)} fusion(f32[512,512]{1,0:T(8,128)S(1)} %get-tuple-element.275, s32[512]{0:T(512)S(1)} %get-tuple-element.259, s32[512]{0:T(512)S(1)} %get-tuple-element.260, s32[512]{0:T(512)S(1)} %get-tuple-element.261, s32[512]{0:T(512)S(1)} %get-tuple-element.262, s32[512]{0:T(512)S(1)} %get-tuple-element.263, ...), kind=kOutput, calls=%fused_computation.3.clone.1 | convolution fusion | flops 273940480 | bytes 2633733 | tf_op jit(solution)/shard_map/while/body/eval_jaxpr/dot_general | solution.py:58
  252.8 5.7 %convolution_add_fusion.6 = f32[512,512]{1,0:T(8,128)S(1)} fusion(f32[512,512]{1,0:T(8,128)S(1)} %get-tuple-element.274, s32[512]{0:T(512)S(1)} %get-tuple-element.259, s32[512]{0:T(512)S(1)} %get-tuple-element.260, s32[512]{0:T(512)S(1)} %get-tuple-element.261, s32[512]{0:T(512)S(1)} %get-tuple-element.262, s32[512]{0:T(512)S(1)} %get-tuple-element.263, ...), kind=kOutput, calls=%fused_computation.4.clone.1 | convolution fusion | flops 273940480 | bytes 2633733 | tf_op jit(solution)/shard_map/while/body/eval_jaxpr/dot_general | solution.py:57
  258.6 5.8 %convolution_add_fusion.7 = f32[512,512]{1,0:T(8,128)S(1)} fusion(f32[512,512]{1,0:T(8,128)S(1)} %get-tuple-element.275, s32[512]{0:T(512)S(1)} %get-tuple-element.259, s32[512]{0:T(512)S(1)} %get-tuple-element.260, s32[512]{0:T(512)S(1)} %get-tuple-element.261, s32[512]{0:T(512)S(1)} %get-tuple-element.262, s32[512]{0:T(512)S(1)} %get-tuple-element.263, ...), kind=kOutput, calls=%fused_computation.3.clone.1 | convolution fusion | flops 273940480 | bytes 2633733 | tf_op jit(solution)/shard_map/while/body/eval_jaxpr/dot_general | solution.py:58
  264.4 5.7 %convolution_add_fusion.6 = f32[512,512]{1,0:T(8,128)S(1)} fusion(f32[512,512]{1,0:T(8,128)S(1)} %get-tuple-element.274, s32[512]{0:T(512)S(1)} %get-tuple-element.259, s32[512]{0:T(512)S(1)} %get-tuple-element.260, s32[512]{0:T(512)S(1)} %get-tuple-element.261, s32[512]{0:T(512)S(1)} %get-tuple-element.262, s32[512]{0:T(512)S(1)} %get-tuple-element.263, ...), kind=kOutput, calls=%fused_computation.4.clone.1 | convolution fusion | flops 273940480 | bytes 2633733 | tf_op jit(solution)/shard_map/while/body/eval_jaxpr/dot_general | solution.py:57
  272.6 20.7 %all-gather.8.cloned.1.call-done = bf16[8,2,64,512]{3,2,0,1:T(8,128)(2,1)} async-done(((bf16[8,2,16,512]{3,2,0,1:T(8,128)(2,1)}), bf16[8,2,64,512]{3,2,0,1:T(8,128)(2,1)}) %all-gather.8.cloned.1.call-update) | async-done | bytes 1048592 | tf_op jit(solution)/shard_map/all_gather | solution.py:123
  293.3 1.4 fusion.46
  294.7 1.3 fusion.30
  300.7 1.3 dynamic-slice
  301.9 187.2 %all-reduce.3.cloned.1.call-done = f32[128,2,64]{2,1,0:T(2,128)} async-done(((f32[128,2,64]{2,1,0:T(2,128)}), f32[128,2,64]{2,1,0:T(2,128)}) %all-reduce.3.cloned.1.call-update) | async-done | bytes 65552
  489.1 1.3 constant_dynamic-slice_fusion
  491.3 17.9 %reduce-scatter.4.cloned.1.call-done = f32[16,2]{1,0:T(8,128)} async-done(((f32[64,2]{1,0:T(8,128)}), f32[16,2]{1,0:T(8,128)}) %reduce-scatter.4.cloned.1.call-update) | async-done | bytes 144
  509.2 0.8 reshape_bitcast_fusion
  (104 shorter events, 15.7 us)
Async XLA Ops:
  6.5 97.6 %all-gather.4.cloned.1.call-start = ((), (), s32[]{:S(2)}) async-start(), calls=%async_computation.1 | async-start | bytes 8454144 | tf_op jit(solution)/shard_map/all_gather | solution.py:89
  7.3 161.7 %all-gather.6.cloned.1.call-start = ((), (), s32[]{:S(2)}) async-start(), calls=%async_computation.2 | async-start | bytes 2621440 | tf_op jit(solution)/shard_map/all_gather | solution.py:109
  123.3 1.0 copy-start.1
  124.2 169.2 %all-gather.8.cloned.1.call-start = ((), (), s32[]{:S(2)}) async-start(), calls=%async_computation.3 | async-start | bytes 1310720 | tf_op jit(solution)/shard_map/all_gather | solution.py:123
  270.2 1.6 copy-start
  271.3 217.8 %all-reduce.3.cloned.1.call-start = ((), (), s32[]{:S(2)}) async-start(), calls=%async_computation.5 | async-start | bytes 262144
  293.3 3.2 copy-start.2
  300.6 208.6 %reduce-scatter.4.cloned.1.call-start = ((), (), s32[]{:S(2)}) async-start(), calls=%async_computation.4 | async-start | bytes 40960
Sparse Core Ops, SparseCore 0:
  10.5 93.6 all-gather.3
  124.3 31.9 all-gather.5
  271.4 21.9 all-gather.7
  300.7 188.3 all-reduce.2
  491.7 17.4 reduce-scatter.3
where the time goes:
time: 520 us; the launch traced here: 517 us
  waiting for transfers between devices  323 us (62%)
  matrix products  103 us (20%)
  blocking collectives  43.5 us (8%)
  local copies, waits for them, and re-layouts  28.3 us (5%)
  between operations  13.6 us (3%)
  other arithmetic  5.79 us (1%)
    unnamed x7, waiting for transfers between devices  206 us
    all_gather x1, waiting for transfers between devices, local(): func_piece = lax.all_gather(band_functions, 'kq', axis=0, tiled=True)  96 us
    dot_general x8, matrix products, add_block(): jnp.dot(piece, sin_table, preferred_element_type=jnp.float32)  46.2 us
    dot_general x8, matrix products, add_block(): jnp.dot(piece, cos_table, preferred_element_type=jnp.float32)  45.9 us
    all_gather x1, blocking collectives, local(): amp_piece = lax.all_gather(exciton, 'kq', axis=0, tiled=True)  43.5 us
    all_gather x1, waiting for transfers between devices, local(): cond_waves = lax.all_gather(cond_waves, 'band', axis=2, tiled=True)  20.7 us
    reshape x1, local copies, waits for them, and re-layouts, local(): func_piece.reshape(piece_rows, -1)  14.5 us
  transfers between devices with their start and end apart: 5, of which 4 were waited for; matrix products, arithmetic and copies ran while one was open for 1% of the time, Pallas kernels for 0%

commit v1 on v0

v1 whole, which is shorter than its diff:
```python
import functools
import math

import jax
import jax.numpy as jnp
import numpy as np
from jax import lax
from jax.experimental import pallas as pl
from jax.experimental.pallas import tpu as pltpu
from jax.sharding import PartitionSpec as P

SIDE = 16
BOX = 8
PLANE = SIDE * SIDE
HALF = BOX * BOX
NG = BOX * HALF
BLOCKS = 4
NT = (((1,), (1,)), ((), ()))


def plane_table():
    y, z = np.divmod(np.arange(PLANE), SIDE)
    gy, gz = np.divmod(np.arange(HALF), BOX)
    m = (y[:, None] * (gy - 4)[None] + z[:, None] * (gz - 4)[None]) % SIDE
    c, s = np.cos(2 * np.pi * m / SIDE), np.sin(2 * np.pi * m / SIDE)
    top = np.concatenate([c, -s, -s, -c], axis=1)
    low = np.concatenate([s, c, c, -s], axis=1)
    return np.concatenate([top, low], axis=0)


def band_of(place):
    return 2 * (place & 3) + (place >> 2)


def weighted(terms):
    total = None
    for factor, value in terms:
        if abs(factor) < 1e-9:
            continue
        if abs(abs(factor) - 1.0) < 1e-9:
            piece = value if factor > 0 else -value
        else:
            piece = value * factor
        total = piece if total is None else total + piece
    return total


def pair_body(
    ints_ref, funcs_ref, screen_ref, table_ref, amps_ref, out_ref, dens, sums, wave_re, wave_im
):
    f32, bf16 = jnp.float32, jnp.bfloat16
    points = amps_ref.shape[0]

    def densities(x, carry):
        tile = [[funcs_ref[(ri * 4 + i) * SIDE + x].astype(f32) for i in range(4)] for ri in range(2)]
        for kind in range(2):
            for s in range(2):

                def bands(ri, base):
                    low, high = tile[ri][2 * kind], tile[ri][2 * kind + 1]
                    return jnp.concatenate([low[base : base + 4], high[base : base + 4]], axis=0)

                left_re, left_im = bands(0, 4 * s)[:, None, :], bands(1, 4 * s)[:, None, :]
                right_re, right_im = bands(0, 8 + 4 * s)[None], bands(1, 8 + 4 * s)[None]
                dens_re = (left_re * right_re + left_im * right_im).reshape(64, PLANE)
                dens_im = (left_re * right_im - left_im * right_re).reshape(64, PLANE)
                row = (kind * 2 + s) * 64
                dens[x, row : row + 64, :PLANE] = dens_re.astype(bf16)
                dens[x, row : row + 64, PLANE:] = dens_im.astype(bf16)
        return carry

    lax.fori_loop(0, SIDE, densities, 0)

    def plane_sums(x, carry):
        sums[x] = jnp.dot(dens[x], table_ref[...], preferred_element_type=f32)
        return carry

    lax.fori_loop(0, SIDE, plane_sums, 0)

    scale = 1.0 / math.sqrt(SIDE**3)
    low_lanes = lax.broadcasted_iota(jnp.int32, (16, 128), 1) < HALF

    def along_x(chunk, carry):
        rows = pl.ds(pl.multiple_of(chunk * 16, 16), 16)
        out = {}
        for parity in range(2):
            sign = 1.0 if parity == 0 else -1.0
            straight, turned = [], []
            for x in range(8):
                straight.append(sums[x, rows, 0:128] + sign * sums[x + 8, rows, 0:128])
                turned.append(sums[x, rows, 128:256] + sign * sums[x + 8, rows, 128:256])
            for g in (0, 2, 4) if parity == 0 else (1, 3):
                angle = [2 * math.pi * x * g / SIDE for x in range(8)]
                even = weighted([(math.cos(a), v) for a, v in zip(angle, straight)])
                odd = weighted([(math.sin(a), v) for a, v in zip(angle, turned)])
                if odd is None:
                    out[-g] = even
                else:
                    out[g], out[-g] = even + odd, even - odd
        for pair in range(4):
            first, second = out[2 * pair - 4] * scale, out[2 * pair - 3] * scale
            re = jnp.where(low_lanes, first, pltpu.roll(second, 64, 1))
            im = jnp.where(low_lanes, pltpu.roll(first, 64, 1), second)
            wave_re[rows, pair * 128 : pair * 128 + 128] = re.astype(bf16)
            wave_im[rows, pair * 128 : pair * 128 + 128] = im.astype(bf16)
        return carry

    lax.fori_loop(0, 16, along_x, 0)

    stacked = jnp.concatenate([wave_re[0:128], wave_im[0:128]], axis=0)
    with_re = lax.dot_general(stacked, screen_ref[0], NT, preferred_element_type=f32)
    with_im = lax.dot_general(stacked, screen_ref[1], NT, preferred_element_type=f32)
    scr_re = (with_re[:128] - with_im[128:]).astype(bf16)
    scr_im = (with_re[128:] + with_im[:128]).astype(bf16)

    here = ints_ref[0]
    second_point = [ints_ref[1], ints_ref[2]]
    first_point = [(here + c) & (points - 1) for c in second_point]
    row8 = lax.broadcasted_iota(jnp.int32, (8, points), 0)
    col8 = lax.broadcasted_iota(jnp.int32, (8, points), 1)
    wanted = jnp.where(
        row8 == 0,
        first_point[0],
        jnp.where(row8 == 1, first_point[1], jnp.where(row8 == 2, second_point[0], second_point[1])),
    )
    chosen = jnp.dot(
        jnp.where(col8 == wanted, 1.0, 0.0).astype(bf16), amps_ref[...], preferred_element_type=f32
    )

    def iota(shape, axis):
        return lax.broadcasted_iota(jnp.int32, shape, axis)

    row, lane = iota((64, 128), 0), iota((64, 128), 1)
    row_hi, row_lo = band_of(row >> 3), band_of(row & 7)
    q, l = iota((128, 64), 0), iota((128, 64), 1)
    q_band = (q & 63) >> 3
    pick_hi = jnp.where(q_band == band_of(l >> 3), 1.0, 0.0).astype(bf16)
    pick_lo = jnp.where(q_band == band_of(l & 7), 1.0, 0.0).astype(bf16)

    def spread(values, row_band, pick):
        kept = jnp.where((lane & 7) == row_band, jnp.broadcast_to(values, (64, 128)), 0.0)
        re = jnp.where(lane < 64, kept, 0.0).astype(bf16)
        im = jnp.where(lane < 64, 0.0, kept).astype(bf16)
        return (
            jnp.dot(re, pick, preferred_element_type=f32),
            jnp.dot(im, pick, preferred_element_type=f32),
        )

    out_band = 2 * (lane >> 5) + ((lane >> 3) & 1)
    out_part = (lane >> 4) & 1
    out_other = lane & 7
    gather_hi = jnp.where(row_hi == out_band, 1.0, 0.0)
    gather_lo = jnp.where(row_lo == out_band, 1.0, 0.0)

    def collect(re, im, gather, row_band):
        dot = functools.partial(
            jnp.dot, precision=lax.Precision.HIGHEST, preferred_element_type=f32
        )
        both = dot(re, jnp.where(out_part == 0, gather, 0.0)) + dot(
            im, jnp.where(out_part == 1, gather, 0.0)
        )
        return jnp.sum(jnp.where(row_band == out_other, both, 0.0), axis=0, keepdims=True)

    k = iota((points, 128), 0)
    total = jnp.zeros((points, 128), f32)
    for s in range(2):
        cond, val = slice(128 + 64 * s, 192 + 64 * s), slice(64 * s, 64 * s + 64)
        cr, ci, sr, si = wave_re[cond], wave_im[cond], scr_re[val], scr_im[val]

        def nt(a, b):
            return lax.dot_general(a, b, NT, preferred_element_type=f32)

        kern_re = (nt(cr, sr) + nt(ci, si)) * (1.0 / NG)
        kern_im = (nt(cr, si) - nt(ci, sr)) * (1.0 / NG)
        far_re, far_im = spread(chosen[2 + s : 3 + s], row_lo, pick_lo)
        near_re, near_im = spread(chosen[s : s + 1], row_hi, pick_hi)
        direct = collect(
            kern_re * far_re - kern_im * far_im,
            kern_re * far_im + kern_im * far_re,
            gather_hi,
            row_hi,
        )
        back = collect(
            kern_re * near_re + kern_im * near_im,
            kern_re * near_im - kern_im * near_re,
            gather_lo,
            row_lo,
        )
        total += jnp.where(k == first_point[s], jnp.broadcast_to(direct, (points, 128)), 0.0)
        total += jnp.where(k == second_point[s], jnp.broadcast_to(back, (points, 128)), 0.0)
    out_ref[...] = total


def pair_terms(ints, funcs, screen, table, amps, interpret=False):
    points = amps.shape[0]
    vmem = pl.BlockSpec(memory_space=pltpu.VMEM)
    return pl.pallas_call(
        pair_body,
        out_shape=jax.ShapeDtypeStruct((points, 128), jnp.float32),
        in_specs=[pl.BlockSpec(memory_space=pltpu.SMEM)] + [vmem] * 4,
        out_specs=vmem,
        scratch_shapes=[
            pltpu.VMEM((SIDE, 256, 2 * PLANE), jnp.bfloat16),
            pltpu.VMEM((SIDE, 256, 4 * HALF), jnp.float32),
            pltpu.VMEM((256, NG), jnp.bfloat16),
            pltpu.VMEM((256, NG), jnp.bfloat16),
        ],
        compiler_params=pltpu.CompilerParams(vmem_limit_bytes=32 << 20),
        name="pair_terms",
        interpret=interpret,
    )(ints, funcs, screen, table, amps)


def local(band_functions, screening, exciton, pair_list):
    bf16 = jnp.bfloat16
    points = lax.axis_size("kq")
    here, block = lax.axis_index("kq"), lax.axis_index("band")
    second = lax.dynamic_slice_in_dim(pair_list[:, 1], 2 * block, 2)

    pieces = band_functions.reshape(points, 2, 128)
    amp_rows = jnp.broadcast_to(exciton.reshape(1, 1, 128), (points, 2, 128))
    held = lax.all_to_all(jnp.concatenate([pieces, amp_rows], axis=1), "kq", 0, 0, tiled=True)
    amps = held[:, 2]
    mine = held[:, :2]
    every = lax.all_to_all(
        jnp.broadcast_to(mine[None], (BLOCKS, points, 2, 128)), "band", 0, 0, tiled=True
    )

    slot = jnp.arange(16, dtype=jnp.int32)
    moved = jnp.where((slot & 4) == 0, second[0], second[1])
    owner = jnp.arange(points, dtype=jnp.int32)
    point = jnp.where(slot[None] < 8, (owner[:, None] + moved[None]) % points, moved[None])
    source = ((slot & 3)[None] * points + point).reshape(-1)
    picker = (source[:, None] == jnp.arange(BLOCKS * points, dtype=jnp.int32)[None]).astype(bf16)
    sent = jnp.dot(picker, every.reshape(BLOCKS * points, PLANE), preferred_element_type=jnp.float32)
    sent = sent.astype(bf16).reshape(points, 16, PLANE)
    funcs = lax.all_to_all(sent, "kq", 0, 0, tiled=True)

    ints = jnp.concatenate([here.astype(jnp.int32)[None], second])
    table = jnp.asarray(plane_table(), dtype=bf16)
    terms = pair_terms(ints, funcs, screening[0], table, amps)
    parts = lax.all_to_all(terms.reshape(points * BLOCKS, 32), ("kq", "band"), 0, 0, tiled=True)
    return jnp.sum(parts, axis=0).reshape(1, 2, 16)


def solution(mesh):
    return jax.shard_map(
        local,
        mesh=mesh,
        in_specs=(
            P("kq", None, "band", None),
            P("kq", None, None, None),
            P("kq", None, None),
            P("kq", None),
        ),
        out_specs=P("kq", None, "band"),
        check_vma=False,
    )
```

time: 520 us -> 121 us (0.23)
  waiting for transfers between devices: 323 us -> 44.9 us
  matrix products: 103 us -> 1.85 us
  starting transfers between devices: 0.39 us -> 30.1 us
  local copies, waits for them, and re-layouts: 28.3 us -> 5.25 us
  blocking collectives: 43.5 us -> 26.8 us
  between operations: 13.6 us -> 0.11 us
  Pallas kernels: 0 us -> 9.15 us
    unnamed x7 -> x0, waiting for transfers between devices: 206 us -> none
    all_gather x3 -> x0, waiting for transfers between devices: 117 us -> none  [the longest x1 96 us: local(): func_piece = lax.all_gather(band_functions, 'kq', axis=0, tiled=True)]
    dot_general x34 -> x1, matrix products: 103 us -> 1.85 us  [local(): jnp.dot(picker, every.reshape(BLOCKS * points, PLANE), preferred_element_...]
    all_to_all x0 -> x3, waiting for transfers between devices: none -> 44.9 us  [the longest x1 30.3 us: local(): funcs = lax.all_to_all(sent, 'kq', 0, 0, tiled=True)]
    all_gather x1 -> x0, blocking collectives: 43.5 us -> none  [local(): amp_piece = lax.all_gather(exciton, 'kq', axis=0, tiled=True)]
    all_to_all x0 -> x3, starting transfers between devices: none -> 30.1 us  [the longest x1 18.4 us: local(): lax.all_to_all(jnp.concatenate([pieces, amp_rows], axis=1), 'kq', 0, 0, t...]
    all_to_all x0 -> x1, blocking collectives: none -> 26.8 us  [local(): lax.all_to_all(terms.reshape(points * BLOCKS, 32), ('kq', 'band'), 0, 0,...]
    reshape x9 -> x2, local copies, waits for them, and re-layouts: 15.6 us -> 1.56 us  [the longest x1 0.92 us: local(): pieces = band_functions.reshape(points, 2, 128)]
  transfers between devices with their start and end apart: 5 -> 3, of which waited for: 4 -> 3; matrix products, arithmetic and copies ran while one was open for 1% -> 3% of each run, Pallas kernels for 0% -> 0%
where the time goes in v1:
time: 121 us
  waiting for transfers between devices  44.9 us (37%)
  starting transfers between devices  30.1 us (25%)
  blocking collectives  26.8 us (22%)
  Pallas kernels  9.15 us (8%)
  local copies, waits for them, and re-layouts  5.25 us (4%)
  other arithmetic  2.73 us (2%)
  matrix products  1.85 us (2%)
    all_to_all x1, waiting for transfers between devices, local(): funcs = lax.all_to_all(sent, 'kq', 0, 0, tiled=True)  30.3 us
    all_to_all x1, blocking collectives, local(): lax.all_to_all(terms.reshape(points * BLOCKS, 32), ('kq', 'band'), 0, 0,...  26.8 us
    all_to_all x1, starting transfers between devices, local(): lax.all_to_all(jnp.concatenate([pieces, amp_rows], axis=1), 'kq', 0, 0, t...  18.4 us
    all_to_all x1, waiting for transfers between devices, local(): lax.all_to_all(jnp.concatenate([pieces, amp_rows], axis=1), 'kq', 0, 0, t...  9.17 us
    pallas_call x1, Pallas kernels, pair_terms(): pl.pallas_call(pair_body, out_shape=jax.ShapeDtypeStruct((points, 128), j...  9.15 us
    all_to_all x1, starting transfers between devices, local(): funcs = lax.all_to_all(sent, 'kq', 0, 0, tiled=True)  7.72 us
    all_to_all x1, waiting for transfers between devices, local(): lax.all_to_all(jnp.broadcast_to(mine[None], (BLOCKS, points, 2, 128)), 'b...  5.52 us
    all_to_all x1, starting transfers between devices, local(): lax.all_to_all(jnp.broadcast_to(mine[None], (BLOCKS, points, 2, 128)), 'b...  4.01 us
  transfers between devices with their start and end apart: 3, of which 3 were waited for; matrix products, arithmetic and copies ran while one was open for 3% of the time, Pallas kernels for 0%

profile of v1, /device:TPU:1, one launch (start us, length us, event | category | flops | bytes accessed | tf_op | source)
XLA Modules:
  0.0 121.0 jit_solution(4486544375079608680)
XLA Ops:
  0.0 0.7 broadcast_in_dim.51
  0.7 0.9 reshape.85
  1.7 0.8 pad_maximum_fusion
  2.5 18.4 %all-to-all-start = ((bf16[128,4,128]{2,1,0:T(4,128)(2,1)}), bf16[128,4,128]{2,1,0:T(4,128)(2,1)S(1)}, u32[]{:S(2)}, u32[]{:S(2)}) async-start(bf16[128,4,128]{2,1,0:T(4,128)(2,1)} %pad_maximum_fusion), calls=%async_computation | async-start | bytes 262144 | tf_op jit(solution)/shard_map/all_to_all | solution.py:222
  20.9 0.7 slice.17
  21.6 0.1 constant_dynamic-slice_fusion
  21.7 0.6 fusion.8
  22.3 0.1 broadcast_in_dim.48
  22.4 1.3 %compare_select_fusion = s32[16]{0:T(128)S(1)} fusion(s32[]{:T(128)} %bitcast.3, s32[]{:T(128)} %bitcast.2), kind=kLoop, calls=%fused_computation.14 | loop fusion | flops 48 | bytes 72 | tf_op jit(solution)/shard_map/jit(_where)/select_n | solution.py:230
  23.7 0.1 add.54
  23.8 0.1 add.50
  23.9 0.1 add.52
  24.0 9.2 %all-to-all-done = bf16[128,4,128]{2,1,0:T(4,128)(2,1)S(1)} async-done(((bf16[128,4,128]{2,1,0:T(4,128)(2,1)}), bf16[128,4,128]{2,1,0:T(4,128)(2,1)S(1)}, u32[]{:S(2)}, u32[]{:S(2)}) %all-to-all-start) | async-done | bytes 131104 | tf_op jit(solution)/shard_map/all_to_all | solution.py:222
  33.2 0.8 broadcast_in_dim.53
  34.0 4.0 %all-to-all-start.1 = ((bf16[4,128,2,128]{3,2,1,0:T(2,128)(2,1)}), bf16[4,128,2,128]{3,2,1,0:T(2,128)(2,1)S(1)}, u32[]{:S(2)}, u32[]{:S(2)}) async-start(bf16[4,128,2,128]{3,2,1,0:T(2,128)(2,1)} %broadcast_in_dim.53), calls=%async_computation.1 | async-start | bytes 524288 | tf_op jit(solution)/shard_map/all_to_all | solution.py:225
  38.1 5.5 %all-to-all-done.1 = bf16[4,128,2,128]{3,2,1,0:T(2,128)(2,1)S(1)} async-done(((bf16[4,128,2,128]{3,2,1,0:T(2,128)(2,1)}), bf16[4,128,2,128]{3,2,1,0:T(2,128)(2,1)S(1)}, u32[]{:S(2)}, u32[]{:S(2)}) %all-to-all-start.1) | async-done | bytes 262176 | tf_op jit(solution)/shard_map/all_to_all | solution.py:225
  43.6 1.8 %fusion.1 = bf16[2048,256]{1,0:T(8,128)(2,1)} fusion(s32[2048]{0:T(1024)S(1)} %fusion.7, bf16[64,8,2,128]{3,2,1,0:T(2,128)(2,1)S(1)} %bitcast.19), kind=kOutput, calls=%fused_computation.2 | convolution fusion | flops 538443776 | bytes 1318912 | tf_op jit(solution)/shard_map/dot_general | solution.py:235
  45.4 0.0 copy-start
  45.4 0.0 copy-start.1
  45.4 7.7 %all-to-all-start.2 = ((bf16[128,16,256]{2,1,0:T(8,128)(2,1)}), bf16[128,16,256]{2,1,0:T(8,128)(2,1)S(1)}, u32[]{:S(2)}, u32[]{:S(2)}) async-start(bf16[128,16,256]{2,1,0:T(8,128)(2,1)} %bitcast.4), calls=%async_computation.2 | async-start | bytes 2097152 | tf_op jit(solution)/shard_map/all_to_all | solution.py:237
  53.2 0.1 fusion.9
  53.3 0.1 pad_add_fusion.ints_ref
  53.3 0.1 slice.23
  53.4 30.3 %all-to-all-done.2.funcs_ref = bf16[128,16,256]{2,1,0:T(8,128)(2,1)S(1)} async-done(((bf16[128,16,256]{2,1,0:T(8,128)(2,1)}), bf16[128,16,256]{2,1,0:T(8,128)(2,1)S(1)}, u32[]{:S(2)}, u32[]{:S(2)}) %all-to-all-start.2) | async-done | bytes 1048608 | tf_op jit(solution)/shard_map/all_to_all | solution.py:237
  83.7 0.0 copy-done
  83.7 0.0 copy-done.1
  83.7 9.2 %pair_terms.1 = f32[128,128]{1,0:T(8,128)S(1)} custom-call(s32[3]{0:T(128)S(1)} %pad_add_fusion.ints_ref, bf16[128,16,256]{2,1,0:T(8,128)(2,1)S(1)} %all-to-all-done.2.funcs_ref, bf16[2,512,512]{2,1,0:T(8,128)(2,1)S(1)} %bitcast.16, bf16[512,256]{1,0:T(8,128)(2,1)S(1)} %copy-done.1, bf16[128,128]{1,0:T(8,128)(2,1)S(1)} %bitcast.17), custom_call_target="tpu_custom_call" | custom-call | tf_op jit(solution)/shard_map/pair_terms/pallas_call | solution.py:197
  92.8 0.1 all_to_all.18
  93.0 26.8 %all_to_all.24 = f32[512,1,32]{2,1,0:T(1,128)S(1)} all-to-all(f32[512,1,32]{2,1,0:T(1,128)S(1)} %bitcast.18), channel_id=1, replica_groups=mesh['kq'=128,'band'=4] {'kq','band'}, dimensions={0} | all-to-all | bytes 131072 | tf_op jit(solution)/shard_map/all_to_all | solution.py:242
  119.8 0.6 reduce_sum.9
  120.3 0.6 reshape.88
  (10 shorter events, 0.1 us)
Async XLA Ops:
  2.5 30.7 %all-to-all-start = ((bf16[128,4,128]{2,1,0:T(4,128)(2,1)}), bf16[128,4,128]{2,1,0:T(4,128)(2,1)S(1)}, u32[]{:S(2)}, u32[]{:S(2)}) async-start(bf16[128,4,128]{2,1,0:T(4,128)(2,1)} %pad_maximum_fusion), calls=%async_computation | async-start | bytes 262144 | tf_op jit(solution)/shard_map/all_to_all | solution.py:222
  34.0 9.5 %all-to-all-start.1 = ((bf16[4,128,2,128]{3,2,1,0:T(2,128)(2,1)}), bf16[4,128,2,128]{3,2,1,0:T(2,128)(2,1)S(1)}, u32[]{:S(2)}, u32[]{:S(2)}) async-start(bf16[4,128,2,128]{3,2,1,0:T(2,128)(2,1)} %broadcast_in_dim.53), calls=%async_computation.1 | async-start | bytes 524288 | tf_op jit(solution)/shard_map/all_to_all | solution.py:225
  45.4 38.2 %copy-start = (bf16[1,2,512,512]{3,2,1,0:T(8,128)(2,1)S(1)}, bf16[1,2,512,512]{3,2,1,0:T(8,128)(2,1)}, u32[]{:S(2)}) copy-start(bf16[1,2,512,512]{3,2,1,0:T(8,128)(2,1)} %param.6) | copy-start | bytes 3145732
  45.4 38.2 %copy-start.1 = (bf16[512,256]{1,0:T(8,128)(2,1)S(1)}, bf16[512,256]{1,0:T(8,128)(2,1)}, u32[]{:S(2)}) copy-start(bf16[512,256]{1,0:T(8,128)(2,1)} %constant.41.clone.table_ref) | copy-start | bytes 786436
  45.4 38.2 %all-to-all-start.2 = ((bf16[128,16,256]{2,1,0:T(8,128)(2,1)}), bf16[128,16,256]{2,1,0:T(8,128)(2,1)S(1)}, u32[]{:S(2)}, u32[]{:S(2)}) async-start(bf16[128,16,256]{2,1,0:T(8,128)(2,1)} %bitcast.4), calls=%async_computation.2 | async-start | bytes 2097152 | tf_op jit(solution)/shard_map/all_to_all | solution.py:237

commit v2 on v1

v2 whole, which is shorter than its diff:
```python
import functools
import math

import jax
import jax.numpy as jnp
import numpy as np
from jax import lax
from jax.experimental import pallas as pl
from jax.experimental.pallas import tpu as pltpu
from jax.sharding import PartitionSpec as P

SIDE = 16
BOX = 8
PLANE = SIDE * SIDE
HALF = BOX * BOX
NG = BOX * HALF
BLOCKS = 4
NT = (((1,), (1,)), ((), ()))


def plane_table():
    y, z = np.divmod(np.arange(PLANE), SIDE)
    gy, gz = np.divmod(np.arange(HALF), BOX)
    m = (y[:, None] * (gy - 4)[None] + z[:, None] * (gz - 4)[None]) % SIDE
    c, s = np.cos(2 * np.pi * m / SIDE), np.sin(2 * np.pi * m / SIDE)
    top = np.concatenate([c, -s, -s, -c], axis=1)
    low = np.concatenate([s, c, c, -s], axis=1)
    return np.concatenate([top, low], axis=0)


def weighted(terms):
    total = None
    for factor, value in terms:
        if abs(factor) < 1e-9:
            continue
        if abs(abs(factor) - 1.0) < 1e-9:
            piece = value if factor > 0 else -value
        else:
            piece = value * factor
        total = piece if total is None else total + piece
    return total


def iota(shape, axis):
    return lax.broadcasted_iota(jnp.int32, shape, axis)


def second_of(seconds_ref, block, parity):
    return seconds_ref[2 * block + parity, 1]


def send_body(pairs_ref, held_ref, sent_ref):
    points = held_ref.shape[0]
    moves = [[second_of(pairs_ref, block, parity) for block in range(BLOCKS)] for parity in range(2)]
    right = [[held_ref[moves[p][b], 0:2] for b in range(BLOCKS)] for p in range(2)]

    def chip(i, carry):
        for parity in range(2):
            for block in range(BLOCKS):
                owner = 2 * i + parity
                target = owner * BLOCKS + block
                other = 2 * i + (1 - parity)
                move = moves[parity][block]
                sent_ref[target, 0] = held_ref[(owner + move) & (points - 1), 0:2]
                sent_ref[target, 1] = held_ref[(other + move) & (points - 1), 0:2]
                sent_ref[target, 2] = right[parity][block]
        return carry

    lax.fori_loop(0, points // 2, chip, 0)


def send_pieces(pairs, held, interpret=False):
    points = held.shape[0]
    vmem = pl.BlockSpec(memory_space=pltpu.VMEM)
    return pl.pallas_call(
        send_body,
        out_shape=jax.ShapeDtypeStruct((points * BLOCKS, 3, 2, 128), jnp.bfloat16),
        in_specs=[pl.BlockSpec(memory_space=pltpu.SMEM), vmem],
        out_specs=vmem,
        name="send_pieces",
        interpret=interpret,
    )(pairs, held)


def pair_body(
    place_ref,
    pairs_ref,
    funcs_ref,
    own_ref,
    other_ref,
    table_ref,
    held_ref,
    out_ref,
    dens,
    sums,
    wave_re,
    wave_im,
):
    f32, bf16 = jnp.float32, jnp.bfloat16
    points = held_ref.shape[0]

    def densities(x, carry):
        for half in range(2):
            lanes = slice(half * 128, half * 128 + 128)
            lanes_im = slice(PLANE + half * 128, PLANE + half * 128 + 128)
            for kind in range(2):

                def bands(ri, slot):
                    piece = (ri * 32 + 2 * x + half) * 2 + kind
                    return funcs_ref[pl.ds(piece * BLOCKS, BLOCKS), slot].astype(f32).reshape(8, 128)

                right_re, right_im = bands(0, 2)[None], bands(1, 2)[None]
                for pair in range(2):
                    left_re, left_im = bands(0, pair)[:, None, :], bands(1, pair)[:, None, :]
                    dens_re = (left_re * right_re + left_im * right_im).reshape(64, 128)
                    dens_im = (left_re * right_im - left_im * right_re).reshape(64, 128)
                    row = (kind * 2 + pair) * 64
                    dens[x, row : row + 64, lanes] = dens_re.astype(bf16)
                    dens[x, row : row + 64, lanes_im] = dens_im.astype(bf16)
        return carry

    lax.fori_loop(0, SIDE, densities, 0)

    def plane_sums(x, carry):
        sums[x] = jnp.dot(dens[x], table_ref[...], preferred_element_type=f32)
        return carry

    lax.fori_loop(0, SIDE, plane_sums, 0)

    scale = 1.0 / math.sqrt(SIDE**3)
    low_lanes = iota((16, 128), 1) < HALF

    def along_x(chunk, carry):
        rows = pl.ds(pl.multiple_of(chunk * 16, 16), 16)
        out = {}
        for parity in range(2):
            sign = 1.0 if parity == 0 else -1.0
            straight, turned = [], []
            for x in range(8):
                straight.append(sums[x, rows, 0:128] + sign * sums[x + 8, rows, 0:128])
                turned.append(sums[x, rows, 128:256] + sign * sums[x + 8, rows, 128:256])
            for g in (0, 2, 4) if parity == 0 else (1, 3):
                angle = [2 * math.pi * x * g / SIDE for x in range(8)]
                even = weighted([(math.cos(a), v) for a, v in zip(angle, straight)])
                odd = weighted([(math.sin(a), v) for a, v in zip(angle, turned)])
                if odd is None:
                    out[-g] = even
                else:
                    out[g], out[-g] = even + odd, even - odd
        for pair in range(4):
            first, second = out[2 * pair - 4] * scale, out[2 * pair - 3] * scale
            re = jnp.where(low_lanes, first, pltpu.roll(second, 64, 1))
            im = jnp.where(low_lanes, pltpu.roll(first, 64, 1), second)
            wave_re[rows, pair * 128 : pair * 128 + 128] = re.astype(bf16)
            wave_im[rows, pair * 128 : pair * 128 + 128] = im.astype(bf16)
        return carry

    lax.fori_loop(0, 16, along_x, 0)

    def nt(a, b):
        return lax.dot_general(a, b, NT, preferred_element_type=f32)

    here, block = place_ref[0], place_ref[1]
    move = second_of(pairs_ref, block, here & 1)
    first_point = [(here + move) & (points - 1), ((here ^ 1) + move) & (points - 1)]

    row, lane = iota((64, 128), 0), iota((64, 128), 1)
    row_hi, row_lo = row >> 3, row & 7
    q, l = iota((128, 64), 0), iota((128, 64), 1)
    pick_hi = jnp.where((q < 64) & ((q >> 3) == (l >> 3)), 1.0, 0.0).astype(bf16)
    pick_lo = jnp.where((q < 64) & ((q >> 3) == (l & 7)), 1.0, 0.0).astype(bf16)

    def spread(point, row_band, pick):
        parts = []
        for ri in range(2):
            values = held_ref[point, 2 + ri : 3 + ri].astype(f32)
            kept = jnp.where((lane & 7) == row_band, jnp.broadcast_to(values, (64, 128)), 0.0)
            parts.append(jnp.dot(kept.astype(bf16), pick, preferred_element_type=f32))
        return parts

    out_band = 2 * (lane >> 5) + ((lane >> 3) & 1)
    out_part = (lane >> 4) & 1
    out_other = lane & 7
    gather_hi = jnp.where(row_hi == out_band, 1.0, 0.0)
    gather_lo = jnp.where(row_lo == out_band, 1.0, 0.0)

    def collect(re, im, gather, row_band):
        dot = functools.partial(
            jnp.dot, precision=lax.Precision.HIGHEST, preferred_element_type=f32
        )
        both = dot(re, jnp.where(out_part == 0, gather, 0.0)) + dot(
            im, jnp.where(out_part == 1, gather, 0.0)
        )
        return jnp.sum(jnp.where(row_band == out_other, both, 0.0), axis=0, keepdims=True)

    far_re, far_im = spread(move, row_lo, pick_lo)
    r = iota((points, 128), 0)
    k = ((r & 7) << 4) | (r >> 3)
    total = jnp.zeros((points, 128), f32)
    back_re = back_im = 0.0
    for pair, weights in enumerate((own_ref, other_ref)):
        val, cond = slice(64 * pair, 64 * pair + 64), slice(128 + 64 * pair, 192 + 64 * pair)
        stacked = jnp.concatenate([wave_re[val], wave_im[val]], axis=0)
        with_re, with_im = nt(stacked, weights[0]), nt(stacked, weights[1])
        scr_re = (with_re[:64] - with_im[64:]).astype(bf16)
        scr_im = (with_re[64:] + with_im[:64]).astype(bf16)
        cond_re, cond_im = wave_re[cond], wave_im[cond]
        kern_re = (nt(cond_re, scr_re) + nt(cond_im, scr_im)) * (1.0 / NG)
        kern_im = (nt(cond_re, scr_im) - nt(cond_im, scr_re)) * (1.0 / NG)
        near_re, near_im = spread(first_point[pair], row_hi, pick_hi)
        direct = collect(
            kern_re * far_re - kern_im * far_im,
            kern_re * far_im + kern_im * far_re,
            gather_hi,
            row_hi,
        )
        back_re += kern_re * near_re + kern_im * near_im
        back_im += kern_re * near_im - kern_im * near_re
        total += jnp.where(k == first_point[pair], jnp.broadcast_to(direct, (points, 128)), 0.0)
    back = collect(back_re, back_im, gather_lo, row_lo)
    total += jnp.where(k == move, jnp.broadcast_to(back, (points, 128)), 0.0)
    out_ref[...] = total


def pair_terms(place, pairs, funcs, own, other, table, held, interpret=False):
    points = held.shape[0]
    vmem, smem = pl.BlockSpec(memory_space=pltpu.VMEM), pl.BlockSpec(memory_space=pltpu.SMEM)
    return pl.pallas_call(
        pair_body,
        out_shape=jax.ShapeDtypeStruct((points, 128), jnp.float32),
        in_specs=[smem, smem] + [vmem] * 5,
        out_specs=vmem,
        scratch_shapes=[
            pltpu.VMEM((SIDE, 256, 2 * PLANE), jnp.bfloat16),
            pltpu.VMEM((SIDE, 256, 4 * HALF), jnp.float32),
            pltpu.VMEM((256, NG), jnp.bfloat16),
            pltpu.VMEM((256, NG), jnp.bfloat16),
        ],
        compiler_params=pltpu.CompilerParams(vmem_limit_bytes=32 << 20),
        name="pair_terms",
        interpret=interpret,
    )(place, pairs, funcs, own, other, table, held)


def local(band_functions, screening, exciton, pair_list):
    bf16 = jnp.bfloat16
    points = lax.axis_size("kq")
    here, block = lax.axis_index("kq"), lax.axis_index("band")
    place = jnp.stack([here, block]).astype(jnp.int32)
    other = lax.ppermute(screening, "kq", [(i, i ^ 1) for i in range(points)])

    pieces = band_functions.reshape(2, 2, 2, 32, 128).transpose(0, 3, 1, 2, 4).reshape(points, 2, 128)
    amp_rows = jnp.pad(exciton, ((0, 0), (0, 0), (0, 64)))
    amp_rows = jnp.broadcast_to(amp_rows, (points, 2, 128))
    held = lax.all_to_all(jnp.concatenate([pieces, amp_rows], axis=1), "kq", 0, 0, tiled=True)

    funcs = lax.all_to_all(send_pieces(pair_list, held), ("kq", "band"), 0, 0, tiled=True)

    table = jnp.asarray(plane_table(), dtype=bf16)
    terms = pair_terms(place, pair_list, funcs, screening[0], other[0], table, held)

    rows = [[16 * y + z for z in range(16)] for y in range(8)]
    columns = [[(16 * y + z) * BLOCKS + b for y in range(8) for b in range(BLOCKS)] for z in range(16)]
    parts = lax.all_to_all(
        terms.reshape(16, 8, 128), "kq", 0, 0, tiled=True, axis_index_groups=rows
    )
    parts = jnp.sum(parts, axis=0).reshape(32, 1, 32)
    parts = lax.all_to_all(
        parts, ("kq", "band"), 0, 0, tiled=True, axis_index_groups=columns
    )
    return jnp.sum(parts, axis=(0, 1)).reshape(1, 2, 16)


def solution(mesh):
    return jax.shard_map(
        local,
        mesh=mesh,
        in_specs=(
            P("kq", None, "band", None),
            P("kq", None, None, None),
            P("kq", None, None),
            P("kq", None),
        ),
        out_specs=P("kq", None, "band"),
        check_vma=False,
    )
```

time: 121 us -> 108 us (0.89)
  waiting for transfers between devices: 44.9 us -> 32.6 us
  starting transfers between devices: 30.1 us -> 34.2 us
  Pallas kernels: 9.15 us -> 13 us
  blocking collectives: 26.8 us -> 24.2 us
  local copies, waits for them, and re-layouts: 5.25 us -> 2.91 us
  matrix products: 1.85 us -> 0 us
  other arithmetic: 2.73 us -> 0.93 us
    all_to_all x2 -> x1, waiting for transfers between devices: 35.8 us -> 18.9 us  [local(): lax.all_to_all(send_pieces(pair_list, held), ('kq', 'band'), 0, 0, tiled=...]
    ppermute x0 -> x1, starting transfers between devices: none -> 6.35 us  [local(): other = lax.ppermute(screening, 'kq', [(i, i ^ 1) for i in range(points)])]
    pallas_call x0 -> x1, Pallas kernels: none -> 3.29 us  [send_pieces(): pl.pallas_call(send_body, out_shape=jax.ShapeDtypeStruct((points * BLOCKS...]
    all_to_all x1 -> x2, blocking collectives: 26.8 us -> 24.2 us  [the longest x1 12.3 us: local(): lax.all_to_all(parts, ('kq', 'band'), 0, 0, tiled=True, axis_index_groups...]
    all_to_all x1, waiting for transfers between devices: 9.17 us -> 11.6 us  [local(): lax.all_to_all(jnp.concatenate([pieces, amp_rows], axis=1), 'kq', 0, 0, t...]
    all_to_all x2 -> x1, starting transfers between devices: 11.7 us -> 9.34 us  [local(): lax.all_to_all(send_pieces(pair_list, held), ('kq', 'band'), 0, 0, tiled=...]
    ppermute x0 -> x1, waiting for transfers between devices: none -> 2.17 us  [local(): other = lax.ppermute(screening, 'kq', [(i, i ^ 1) for i in range(points)])]
    dot_general x1 -> x0, matrix products: 1.85 us -> none  [local(): jnp.dot(picker, every.reshape(BLOCKS * points, PLANE), preferred_element_...]
  transfers between devices with their start and end apart: 3 -> 3, of which waited for: 3 -> 3; matrix products, arithmetic and copies ran while one was open for 3% -> 1% of each run, Pallas kernels for 0% -> 0%
where the time goes in v2:
time: 108 us
  starting transfers between devices  34.2 us (32%)
  waiting for transfers between devices  32.6 us (30%)
  blocking collectives  24.2 us (22%)
  Pallas kernels  13 us (12%)
  local copies, waits for them, and re-layouts  2.91 us (3%)
    all_to_all x1, waiting for transfers between devices, local(): lax.all_to_all(send_pieces(pair_list, held), ('kq', 'band'), 0, 0, tiled=...  18.9 us
    all_to_all x1, starting transfers between devices, local(): lax.all_to_all(jnp.concatenate([pieces, amp_rows], axis=1), 'kq', 0, 0, t...  18.5 us
    all_to_all x1, blocking collectives, local(): lax.all_to_all(parts, ('kq', 'band'), 0, 0, tiled=True, axis_index_groups...  12.3 us
    all_to_all x1, blocking collectives, local(): lax.all_to_all(terms.reshape(16, 8, 128), 'kq', 0, 0, tiled=True, axis_in...  11.9 us
    all_to_all x1, waiting for transfers between devices, local(): lax.all_to_all(jnp.concatenate([pieces, amp_rows], axis=1), 'kq', 0, 0, t...  11.6 us
    pallas_call x1, Pallas kernels, pair_terms(): pl.pallas_call(pair_body, out_shape=jax.ShapeDtypeStruct((points, 128), j...  9.75 us
    all_to_all x1, starting transfers between devices, local(): lax.all_to_all(send_pieces(pair_list, held), ('kq', 'band'), 0, 0, tiled=...  9.34 us
    ppermute x1, starting transfers between devices, local(): other = lax.ppermute(screening, 'kq', [(i, i ^ 1) for i in range(points)])  6.35 us
  transfers between devices with their start and end apart: 3, of which 3 were waited for; matrix products, arithmetic and copies ran while one was open for 1% of the time, Pallas kernels for 0%

profile of v2, /device:TPU:1, one launch (start us, length us, event | category | flops | bytes accessed | tf_op | source)
XLA Modules:
  0.0 108.0 jit_solution(3180405945108923932)
XLA Ops:
  0.0 0.0 copy-start.5
  0.0 0.7 pad_bitcast_fusion
  0.7 0.1 copy-done.5
  0.8 0.8 pad_maximum_fusion
  1.6 0.0 copy-start.6
  1.6 18.5 %all-to-all-start = ((bf16[128,4,128]{2,1,0:T(4,128)(2,1)}), bf16[128,4,128]{2,1,0:T(4,128)(2,1)S(1)}, u32[]{:S(2)}, u32[]{:S(2)}) async-start(bf16[128,4,128]{2,1,0:T(4,128)(2,1)} %pad_maximum_fusion), calls=%async_computation | async-start | bytes 262144 | tf_op jit(solution)/shard_map/all_to_all | solution.py:255
  20.2 0.0 copy-done.6
  20.2 0.7 copy.11.pairs_ref
  20.9 0.0 copy-start.2
  20.9 11.6 %all-to-all-done.held_ref = bf16[128,4,128]{2,1,0:T(4,128)(2,1)S(1)} async-done(((bf16[128,4,128]{2,1,0:T(4,128)(2,1)}), bf16[128,4,128]{2,1,0:T(4,128)(2,1)S(1)}, u32[]{:S(2)}, u32[]{:S(2)}) %all-to-all-start) | async-done | bytes 131104 | tf_op jit(solution)/shard_map/all_to_all | solution.py:255
  32.4 0.0 copy-start
  32.4 0.7 copy-done
  33.1 3.3 %send_pieces.1 = bf16[512,3,2,128]{3,2,1,0:T(2,128)(2,1)} custom-call(s32[8,2]{1,0:T(8,128)} %copy.11.pairs_ref, bf16[128,4,128]{2,1,0:T(4,128)(2,1)} %copy-done), custom_call_target="tpu_custom_call" | custom-call | tf_op jit(solution)/shard_map/send_pieces/pallas_call | solution.py:75
  36.4 0.0 copy-start.1
  36.4 0.0 copy-start.3
  36.4 9.3 %all-to-all-start.1 = ((bf16[512,3,2,128]{3,2,1,0:T(2,128)(2,1)}), bf16[512,3,2,128]{3,2,1,0:T(2,128)(2,1)S(1)}, u32[]{:S(2)}, u32[]{:S(2)}) async-start(bf16[512,3,2,128]{3,2,1,0:T(2,128)(2,1)} %send_pieces.1), calls=%async_computation.1 | async-start | bytes 1572864 | tf_op jit(solution)/shard_map/all_to_all | solution.py:257
  45.7 0.0 copy-done.2
  45.7 6.3 %collective-permute-start = (bf16[1,2,512,512]{3,2,1,0:T(8,128)(2,1)S(1)}, bf16[1,2,512,512]{3,2,1,0:T(8,128)(2,1)S(1)}, u32[]{:S(2)}, u32[]{:S(2)}) collective-permute-start(bf16[1,2,512,512]{3,2,1,0:T(8,128)(2,1)S(1)} %copy-done.2), channel_id=1, source_target_pairs={{0,4},{4,0},{8,12},{12,8},{16,20},{20,16},{24,28},{28,24},{32,36},... | collective-permute-start | bytes 3145736 | tf_op jit(solution)/shard_map/ppermute | solution.py:250
  52.1 0.0 copy-start.4
  52.1 0.1 pad_add_fusion.place_ref
  52.2 2.2 %collective-permute-done = bf16[1,2,512,512]{3,2,1,0:T(8,128)(2,1)S(1)} collective-permute-done((bf16[1,2,512,512]{3,2,1,0:T(8,128)(2,1)S(1)}, bf16[1,2,512,512]{3,2,1,0:T(8,128)(2,1)S(1)}, u32[]{:S(2)}, u32[]{:S(2)}) %collective-permute-start) | collective-permute-done | bytes 1048608 | tf_op jit(solution)/shard_map/ppermute | solution.py:250
  54.4 18.9 %all-to-all-done.1.funcs_ref = bf16[512,3,2,128]{3,2,1,0:T(2,128)(2,1)S(1)} async-done(((bf16[512,3,2,128]{3,2,1,0:T(2,128)(2,1)}), bf16[512,3,2,128]{3,2,1,0:T(2,128)(2,1)S(1)}, u32[]{:S(2)}, u32[]{:S(2)}) %all-to-all-start.1) | async-done | bytes 786464 | tf_op jit(solution)/shard_map/all_to_all | solution.py:257
  73.2 0.0 copy-done.1
  73.2 0.0 copy-done.3
  73.2 0.0 copy-done.4
  73.2 9.7 %pair_terms.1 = f32[128,128]{1,0:T(8,128)S(1)} custom-call(s32[2]{0:T(128)S(1)} %pad_add_fusion.place_ref, s32[8,2]{1,0:T(8,128)S(1)} %copy-done.4, bf16[512,3,2,128]{3,2,1,0:T(2,128)(2,1)S(1)} %all-to-all-done.1.funcs_ref, bf16[2,512,512]{2,1,0:T(8,128)(2,1)S(1)} %bitcast.12, bf16[2,512,512]{2,1,0:T(8,128)(2,1)S(1)} %bitcast.13, ...), custom_call_target="tpu_custom_call" | custom-call | tf_op jit(solution)/shard_map/pair_terms/pallas_call | solution.py:228
  83.0 11.9 %all_to_all.20 = f32[16,8,128]{2,1,0:T(8,128)S(1)} all-to-all(f32[16,8,128]{2,1,0:T(8,128)S(1)} %bitcast.14), channel_id=1, replica_groups={{0,4,8,12,16,20,24,28,32,36,40,44,48,52,56,60},{64,68,72,76,80,84,88,92..., dimensions={0} | all-to-all | bytes 131072 | tf_op jit(solution)/shard_map/all_to_all | solution.py:264
  94.9 0.1 reshape.18
  95.0 12.3 %all_to_all.21 = f32[32,1,32]{2,1,0:T(1,128)S(1)} all-to-all(f32[32,1,32]{2,1,0:T(1,128)S(1)} %reshape.18), channel_id=1, replica_groups={{0,1,2,3,64,65,66,67,128,129,130,131,192,193,194,195,256,257,258,259,32..., dimensions={0} | all-to-all | bytes 8192 | tf_op jit(solution)/shard_map/all_to_all | solution.py:268
  107.3 0.1 reduce_sum.19
  107.4 0.6 reshape.19
  (2 shorter events, 0.1 us)
Async XLA Ops:
  0.0 0.8 copy-start.5
  1.6 18.6 %copy-start.6 = (s32[8,2]{0,1:T(2,128)S(1)}, s32[8,2]{0,1:T(2,128)}, u32[]{:S(2)}) copy-start(s32[8,2]{0,1:T(2,128)} %param.8) | copy-start | bytes 196
  1.6 30.8 %all-to-all-start = ((bf16[128,4,128]{2,1,0:T(4,128)(2,1)}), bf16[128,4,128]{2,1,0:T(4,128)(2,1)S(1)}, u32[]{:S(2)}, u32[]{:S(2)}) async-start(bf16[128,4,128]{2,1,0:T(4,128)(2,1)} %pad_maximum_fusion), calls=%async_computation | async-start | bytes 262144 | tf_op jit(solution)/shard_map/all_to_all | solution.py:255
  20.9 24.9 %copy-start.2 = (bf16[1,2,512,512]{3,2,1,0:T(8,128)(2,1)S(1)}, bf16[1,2,512,512]{3,2,1,0:T(8,128)(2,1)}, u32[]{:S(2)}) copy-start(bf16[1,2,512,512]{3,2,1,0:T(8,128)(2,1)} %param.6) | copy-start | bytes 3145732
  32.4 0.7 copy-start
  36.4 36.9 %copy-start.1 = (bf16[128,4,128]{2,1,0:T(4,128)(2,1)S(1)}, bf16[128,4,128]{2,1,0:T(4,128)(2,1)}, u32[]{:S(2)}) copy-start(bf16[128,4,128]{2,1,0:T(4,128)(2,1)} %copy-done) | copy-start | bytes 393220
  36.4 36.9 %copy-start.3 = (bf16[512,256]{1,0:T(8,128)(2,1)S(1)}, bf16[512,256]{1,0:T(8,128)(2,1)}, u32[]{:S(2)}) copy-start(bf16[512,256]{1,0:T(8,128)(2,1)} %constant.16.clone.table_ref) | copy-start | bytes 786436
  36.4 36.9 %all-to-all-start.1 = ((bf16[512,3,2,128]{3,2,1,0:T(2,128)(2,1)}), bf16[512,3,2,128]{3,2,1,0:T(2,128)(2,1)S(1)}, u32[]{:S(2)}, u32[]{:S(2)}) async-start(bf16[512,3,2,128]{3,2,1,0:T(2,128)(2,1)} %send_pieces.1), calls=%async_computation.1 | async-start | bytes 1572864 | tf_op jit(solution)/shard_map/all_to_all | solution.py:257
  45.7 8.6 %collective-permute-start = (bf16[1,2,512,512]{3,2,1,0:T(8,128)(2,1)S(1)}, bf16[1,2,512,512]{3,2,1,0:T(8,128)(2,1)S(1)}, u32[]{:S(2)}, u32[]{:S(2)}) collective-permute-start(bf16[1,2,512,512]{3,2,1,0:T(8,128)(2,1)S(1)} %copy-done.2), channel_id=1, source_target_pairs={{0,4},{4,0},{8,12},{12,8},{16,20},{20,16},{24,28},{28,24},{32,36},... | collective-permute-start | bytes 3145736 | tf_op jit(solution)/shard_map/ppermute | solution.py:250
  52.1 21.1 %copy-start.4 = (s32[8,2]{1,0:T(8,128)S(1)}, s32[8,2]{1,0:T(8,128)}, u32[]{:S(2)}) copy-start(s32[8,2]{1,0:T(8,128)} %copy.11.pairs_ref) | copy-start | bytes 196

commit v3 on v2

--- a/solution.py
+++ b/solution.py
@@ -49,24 +49,45 @@
     return seconds_ref[2 * block + parity, 1]
 
 
-def send_body(pairs_ref, held_ref, sent_ref):
+def pack_body(pieces_ref, exciton_ref, packed_ref):
+    points = pieces_ref.shape[0]
+    amps = jnp.concatenate([exciton_ref[0], jnp.zeros((2, 64), jnp.bfloat16)], axis=1)
+    packed_ref[:, 0:2] = pieces_ref[...]
+    packed_ref[:, 2:4] = jnp.broadcast_to(amps[None], (points, 2, 128))
+
+
+def pack_pieces(pieces, exciton, interpret=False):
+    points = pieces.shape[0]
+    vmem = pl.BlockSpec(memory_space=pltpu.VMEM)
+    return pl.pallas_call(
+        pack_body,
+        out_shape=jax.ShapeDtypeStruct((points, 4, 128), jnp.bfloat16),
+        in_specs=[vmem, vmem],
+        out_specs=vmem,
+        compiler_params=pltpu.CompilerParams(vmem_limit_bytes=4 << 20),
+        name="pack_pieces",
+        interpret=interpret,
+    )(pieces, exciton)
+
+
+def send_body(pairs_ref, held_ref, sent_ref, twice):
     points = held_ref.shape[0]
+    twice[0:points] = held_ref[...]
+    twice[points : 2 * points] = held_ref[...]
     moves = [[second_of(pairs_ref, block, parity) for block in range(BLOCKS)] for parity in range(2)]
     right = [[held_ref[moves[p][b], 0:2] for b in range(BLOCKS)] for p in range(2)]
 
     def chip(i, carry):
         for parity in range(2):
             for block in range(BLOCKS):
-                owner = 2 * i + parity
-                target = owner * BLOCKS + block
-                other = 2 * i + (1 - parity)
-                move = moves[parity][block]
-                sent_ref[target, 0] = held_ref[(owner + move) & (points - 1), 0:2]
-                sent_ref[target, 1] = held_ref[(other + move) & (points - 1), 0:2]
+                target = (2 * i + parity) * BLOCKS + block
+                run = 2 * i + moves[parity][block]
+                sent_ref[target, 0] = twice[run + parity, 0:2]
+                sent_ref[target, 1] = twice[run + (1 - parity), 0:2]
                 sent_ref[target, 2] = right[parity][block]
         return carry
 
-    lax.fori_loop(0, points // 2, chip, 0)
+    lax.fori_loop(0, points // 2, chip, 0, unroll=2)
 
 
 def send_pieces(pairs, held, interpret=False):
@@ -77,6 +98,8 @@
         out_shape=jax.ShapeDtypeStruct((points * BLOCKS, 3, 2, 128), jnp.bfloat16),
         in_specs=[pl.BlockSpec(memory_space=pltpu.SMEM), vmem],
         out_specs=vmem,
+        scratch_shapes=[pltpu.VMEM((2 * points, 4, 128), jnp.bfloat16)],
+        compiler_params=pltpu.CompilerParams(vmem_limit_bytes=4 << 20),
         name="send_pieces",
         interpret=interpret,
     )(pairs, held)
@@ -91,7 +114,8 @@
     table_ref,
     held_ref,
     out_ref,
-    dens,
+    dens_even,
+    dens_odd,
     sums,
     wave_re,
     wave_im,
@@ -99,7 +123,7 @@
     f32, bf16 = jnp.float32, jnp.bfloat16
     points = held_ref.shape[0]
 
-    def densities(x, carry):
+    def densities(x, dens):
         for half in range(2):
             lanes = slice(half * 128, half * 128 + 128)
             lanes_im = slice(PLANE + half * 128, PLANE + half * 128 + 128)
@@ -115,17 +139,20 @@
                     dens_re = (left_re * right_re + left_im * right_im).reshape(64, 128)
                     dens_im = (left_re * right_im - left_im * right_re).reshape(64, 128)
                     row = (kind * 2 + pair) * 64
-                    dens[x, row : row + 64, lanes] = dens_re.astype(bf16)
-                    dens[x, row : row + 64, lanes_im] = dens_im.astype(bf16)
+                    dens[row : row + 64, lanes] = dens_re.astype(bf16)
+                    dens[row : row + 64, lanes_im] = dens_im.astype(bf16)
+
+    densities(0, dens_even)
+
+    def planes(i, carry):
+        x = 2 * i
+        sums[x] = jnp.dot(dens_even[...], table_ref[...], preferred_element_type=f32)
+        densities(x + 1, dens_odd)
+        sums[x + 1] = jnp.dot(dens_odd[...], table_ref[...], preferred_element_type=f32)
+        densities(jnp.minimum(x + 2, SIDE - 1), dens_even)
         return carry
 
-    lax.fori_loop(0, SIDE, densities, 0)
-
-    def plane_sums(x, carry):
-        sums[x] = jnp.dot(dens[x], table_ref[...], preferred_element_type=f32)
-        return carry
-
-    lax.fori_loop(0, SIDE, plane_sums, 0)
+    lax.fori_loop(0, SIDE // 2, planes, 0)
 
     scale = 1.0 / math.sqrt(SIDE**3)
     low_lanes = iota((16, 128), 1) < HALF
@@ -231,7 +258,8 @@
         in_specs=[smem, smem] + [vmem] * 5,
         out_specs=vmem,
         scratch_shapes=[
-            pltpu.VMEM((SIDE, 256, 2 * PLANE), jnp.bfloat16),
+            pltpu.VMEM((256, 2 * PLANE), jnp.bfloat16),
+            pltpu.VMEM((256, 2 * PLANE), jnp.bfloat16),
             pltpu.VMEM((SIDE, 256, 4 * HALF), jnp.float32),
             pltpu.VMEM((256, NG), jnp.bfloat16),
             pltpu.VMEM((256, NG), jnp.bfloat16),
@@ -250,9 +278,7 @@
     other = lax.ppermute(screening, "kq", [(i, i ^ 1) for i in range(points)])
 
     pieces = band_functions.reshape(2, 2, 2, 32, 128).transpose(0, 3, 1, 2, 4).reshape(points, 2, 128)
-    amp_rows = jnp.pad(exciton, ((0, 0), (0, 0), (0, 64)))
-    amp_rows = jnp.broadcast_to(amp_rows, (points, 2, 128))
-    held = lax.all_to_all(jnp.concatenate([pieces, amp_rows], axis=1), "kq", 0, 0, tiled=True)
+    held = lax.all_to_all(pack_pieces(pieces, exciton), "kq", 0, 0, tiled=True)
 
     funcs = lax.all_to_all(send_pieces(pair_list, held), ("kq", "band"), 0, 0, tiled=True)
 

time: 108 us -> 105 us (0.972)
  Pallas kernels: 13 us -> 10.8 us
    pallas_call x1, Pallas kernels: 9.75 us -> 7.85 us  [pair_terms(): pl.pallas_call(pair_body, out_shape=jax.ShapeDtypeStruct((points, 128), j...]
  transfers between devices with their start and end apart: 3 -> 3, of which waited for: 3 -> 3; matrix products, arithmetic and copies ran while one was open for 1% -> 0% of each run, Pallas kernels for 0% -> 0%
where the time goes in v3:
time: 105 us
  starting transfers between devices  34.2 us (33%)
  waiting for transfers between devices  33.2 us (32%)
  blocking collectives  24.2 us (23%)
  Pallas kernels  10.8 us (10%)
  local copies, waits for them, and re-layouts  2.32 us (2%)
    all_to_all x1, waiting for transfers between devices, local(): lax.all_to_all(send_pieces(pair_list, held), ('kq', 'band'), 0, 0, tiled=...  18.9 us
    all_to_all x1, starting transfers between devices, local(): held = lax.all_to_all(pack_pieces(pieces, exciton), 'kq', 0, 0, tiled=True)  18.5 us
    all_to_all x1, blocking collectives, local(): lax.all_to_all(parts, ('kq', 'band'), 0, 0, tiled=True, axis_index_groups...  12.3 us
    all_to_all x1, waiting for transfers between devices, local(): held = lax.all_to_all(pack_pieces(pieces, exciton), 'kq', 0, 0, tiled=True)  12.2 us
    all_to_all x1, blocking collectives, local(): lax.all_to_all(terms.reshape(16, 8, 128), 'kq', 0, 0, tiled=True, axis_in...  11.9 us
    all_to_all x1, starting transfers between devices, local(): lax.all_to_all(send_pieces(pair_list, held), ('kq', 'band'), 0, 0, tiled=...  9.31 us
    pallas_call x1, Pallas kernels, pair_terms(): pl.pallas_call(pair_body, out_shape=jax.ShapeDtypeStruct((points, 128), j...  7.85 us
    ppermute x1, starting transfers between devices, local(): other = lax.ppermute(screening, 'kq', [(i, i ^ 1) for i in range(points)])  6.35 us
  transfers between devices with their start and end apart: 3, of which 3 were waited for; matrix products, arithmetic and copies ran while one was open for 0% of the time, Pallas kernels for 0%

profile of v3, /device:TPU:1, one launch (start us, length us, event | category | flops | bytes accessed | tf_op | source)
XLA Modules:
  0.0 105.0 jit_solution(1600303155393886098)
XLA Ops:
  0.0 0.0 copy-start.3
  0.0 0.7 copy-done.3
  0.7 0.0 copy-start.2
  0.7 0.8 copy-done.2
  1.5 0.7 pack_pieces.1
  2.2 0.0 copy-start.4
  2.2 18.5 %all-to-all-start = ((bf16[128,4,128]{2,1,0:T(4,128)(2,1)}), bf16[128,4,128]{2,1,0:T(4,128)(2,1)S(1)}, u32[]{:S(2)}, u32[]{:S(2)}) async-start(bf16[128,4,128]{2,1,0:T(4,128)(2,1)} %pack_pieces.1), calls=%async_computation | async-start | bytes 262144 | tf_op jit(solution)/shard_map/all_to_all | solution.py:281
  20.8 0.0 copy-done.4
  20.8 0.1 copy.11.pairs_ref
  20.9 0.0 copy-start
  20.9 12.2 %all-to-all-done.held_ref = bf16[128,4,128]{2,1,0:T(4,128)(2,1)S(1)} async-done(((bf16[128,4,128]{2,1,0:T(4,128)(2,1)}), bf16[128,4,128]{2,1,0:T(4,128)(2,1)S(1)}, u32[]{:S(2)}, u32[]{:S(2)}) %all-to-all-start) | async-done | bytes 131104 | tf_op jit(solution)/shard_map/all_to_all | solution.py:281
  33.0 2.3 %send_pieces.1 = bf16[512,3,2,128]{3,2,1,0:T(2,128)(2,1)} custom-call(s32[8,2]{1,0:T(8,128)S(1)} %copy.11.pairs_ref, bf16[128,4,128]{2,1,0:T(4,128)(2,1)S(1)} %all-to-all-done.held_ref), custom_call_target="tpu_custom_call" | custom-call | tf_op jit(solution)/shard_map/send_pieces/pallas_call | solution.py:96
  35.3 0.0 copy-start.1
  35.3 9.3 %all-to-all-start.1 = ((bf16[512,3,2,128]{3,2,1,0:T(2,128)(2,1)}), bf16[512,3,2,128]{3,2,1,0:T(2,128)(2,1)S(1)}, u32[]{:S(2)}, u32[]{:S(2)}) async-start(bf16[512,3,2,128]{3,2,1,0:T(2,128)(2,1)} %send_pieces.1), calls=%async_computation.1 | async-start | bytes 1572864 | tf_op jit(solution)/shard_map/all_to_all | solution.py:283
  44.6 0.0 copy-done
  44.6 6.3 %collective-permute-start = (bf16[1,2,512,512]{3,2,1,0:T(8,128)(2,1)S(1)}, bf16[1,2,512,512]{3,2,1,0:T(8,128)(2,1)S(1)}, u32[]{:S(2)}, u32[]{:S(2)}) collective-permute-start(bf16[1,2,512,512]{3,2,1,0:T(8,128)(2,1)S(1)} %copy-done), channel_id=1, source_target_pairs={{0,4},{4,0},{8,12},{12,8},{16,20},{20,16},{24,28},{28,24},{32,36},... | collective-permute-start | bytes 3145736 | tf_op jit(solution)/shard_map/ppermute | solution.py:278
  51.0 0.1 pad_add_fusion.place_ref
  51.1 2.2 %collective-permute-done = bf16[1,2,512,512]{3,2,1,0:T(8,128)(2,1)S(1)} collective-permute-done((bf16[1,2,512,512]{3,2,1,0:T(8,128)(2,1)S(1)}, bf16[1,2,512,512]{3,2,1,0:T(8,128)(2,1)S(1)}, u32[]{:S(2)}, u32[]{:S(2)}) %collective-permute-start) | collective-permute-done | bytes 1048608 | tf_op jit(solution)/shard_map/ppermute | solution.py:278
  53.3 18.9 %all-to-all-done.1.funcs_ref = bf16[512,3,2,128]{3,2,1,0:T(2,128)(2,1)S(1)} async-done(((bf16[512,3,2,128]{3,2,1,0:T(2,128)(2,1)}), bf16[512,3,2,128]{3,2,1,0:T(2,128)(2,1)S(1)}, u32[]{:S(2)}, u32[]{:S(2)}) %all-to-all-start.1) | async-done | bytes 786464 | tf_op jit(solution)/shard_map/all_to_all | solution.py:283
  72.1 0.0 copy-done.1
  72.1 7.8 %pair_terms.1 = f32[128,128]{1,0:T(8,128)S(1)} custom-call(s32[2]{0:T(128)S(1)} %pad_add_fusion.place_ref, s32[8,2]{1,0:T(8,128)S(1)} %copy.11.pairs_ref, bf16[512,3,2,128]{3,2,1,0:T(2,128)(2,1)S(1)} %all-to-all-done.1.funcs_ref, bf16[2,512,512]{2,1,0:T(8,128)(2,1)S(1)} %bitcast.10, bf16[2,512,512]{2,1,0:T(8,128)(2,1)S(1)} %bitcast.11, ...), custom_call_target="tpu_custom_call" | custom-call | tf_op jit(solution)/shard_map/pair_terms/pallas_call | solution.py:255
  80.0 11.9 %all_to_all.20 = f32[16,8,128]{2,1,0:T(8,128)S(1)} all-to-all(f32[16,8,128]{2,1,0:T(8,128)S(1)} %bitcast.12), channel_id=1, replica_groups={{0,4,8,12,16,20,24,28,32,36,40,44,48,52,56,60},{64,68,72,76,80,84,88,92..., dimensions={0} | all-to-all | bytes 131072 | tf_op jit(solution)/shard_map/all_to_all | solution.py:290
  91.9 0.1 reshape.18
  92.0 12.3 %all_to_all.21 = f32[32,1,32]{2,1,0:T(1,128)S(1)} all-to-all(f32[32,1,32]{2,1,0:T(1,128)S(1)} %reshape.18), channel_id=1, replica_groups={{0,1,2,3,64,65,66,67,128,129,130,131,192,193,194,195,256,257,258,259,32..., dimensions={0} | all-to-all | bytes 8192 | tf_op jit(solution)/shard_map/all_to_all | solution.py:294
  104.3 0.1 reduce_sum.19
  104.4 0.6 reshape.19
  (1 shorter events, 0.0 us)
Async XLA Ops:
  0.0 0.7 copy-start.3
  0.7 0.8 copy-start.2
  2.2 18.6 %copy-start.4 = (s32[8,2]{0,1:T(2,128)S(1)}, s32[8,2]{0,1:T(2,128)}, u32[]{:S(2)}) copy-start(s32[8,2]{0,1:T(2,128)} %param.8) | copy-start | bytes 196
  2.2 30.8 %all-to-all-start = ((bf16[128,4,128]{2,1,0:T(4,128)(2,1)}), bf16[128,4,128]{2,1,0:T(4,128)(2,1)S(1)}, u32[]{:S(2)}, u32[]{:S(2)}) async-start(bf16[128,4,128]{2,1,0:T(4,128)(2,1)} %pack_pieces.1), calls=%async_computation | async-start | bytes 262144 | tf_op jit(solution)/shard_map/all_to_all | solution.py:281
  20.9 23.8 %copy-start = (bf16[1,2,512,512]{3,2,1,0:T(8,128)(2,1)S(1)}, bf16[1,2,512,512]{3,2,1,0:T(8,128)(2,1)}, u32[]{:S(2)}) copy-start(bf16[1,2,512,512]{3,2,1,0:T(8,128)(2,1)} %param.6) | copy-start | bytes 3145732
  35.3 36.8 %copy-start.1 = (bf16[512,256]{1,0:T(8,128)(2,1)S(1)}, bf16[512,256]{1,0:T(8,128)(2,1)}, u32[]{:S(2)}) copy-start(bf16[512,256]{1,0:T(8,128)(2,1)} %constant.13.clone.table_ref) | copy-start | bytes 786436
  35.3 36.8 %all-to-all-start.1 = ((bf16[512,3,2,128]{3,2,1,0:T(2,128)(2,1)}), bf16[512,3,2,128]{3,2,1,0:T(2,128)(2,1)S(1)}, u32[]{:S(2)}, u32[]{:S(2)}) async-start(bf16[512,3,2,128]{3,2,1,0:T(2,128)(2,1)} %send_pieces.1), calls=%async_computation.1 | async-start | bytes 1572864 | tf_op jit(solution)/shard_map/all_to_all | solution.py:283
  44.6 8.6 %collective-permute-start = (bf16[1,2,512,512]{3,2,1,0:T(8,128)(2,1)S(1)}, bf16[1,2,512,512]{3,2,1,0:T(8,128)(2,1)S(1)}, u32[]{:S(2)}, u32[]{:S(2)}) collective-permute-start(bf16[1,2,512,512]{3,2,1,0:T(8,128)(2,1)S(1)} %copy-done), channel_id=1, source_target_pairs={{0,4},{4,0},{8,12},{12,8},{16,20},{20,16},{24,28},{28,24},{32,36},... | collective-permute-start | bytes 3145736 | tf_op jit(solution)/shard_map/ppermute | solution.py:278

commit v4 on v3

--- a/solution.py
+++ b/solution.py
@@ -64,7 +64,6 @@
         out_shape=jax.ShapeDtypeStruct((points, 4, 128), jnp.bfloat16),
         in_specs=[vmem, vmem],
         out_specs=vmem,
-        compiler_params=pltpu.CompilerParams(vmem_limit_bytes=4 << 20),
         name="pack_pieces",
         interpret=interpret,
     )(pieces, exciton)
@@ -116,6 +115,8 @@
     out_ref,
     dens_even,
     dens_odd,
+    left_even,
+    left_odd,
     sums,
     wave_re,
     wave_im,
@@ -123,33 +124,39 @@
     f32, bf16 = jnp.float32, jnp.bfloat16
     points = held_ref.shape[0]
 
-    def densities(x, dens):
-        for half in range(2):
-            lanes = slice(half * 128, half * 128 + 128)
-            lanes_im = slice(PLANE + half * 128, PLANE + half * 128 + 128)
-            for kind in range(2):
-
-                def bands(ri, slot):
+    def densities(x, dens, left):
+        for kind in range(2):
+
+            def bands(ri, slot):
+                parts = []
+                for half in range(2):
                     piece = (ri * 32 + 2 * x + half) * 2 + kind
-                    return funcs_ref[pl.ds(piece * BLOCKS, BLOCKS), slot].astype(f32).reshape(8, 128)
-
-                right_re, right_im = bands(0, 2)[None], bands(1, 2)[None]
-                for pair in range(2):
-                    left_re, left_im = bands(0, pair)[:, None, :], bands(1, pair)[:, None, :]
-                    dens_re = (left_re * right_re + left_im * right_im).reshape(64, 128)
-                    dens_im = (left_re * right_im - left_im * right_re).reshape(64, 128)
-                    row = (kind * 2 + pair) * 64
-                    dens[row : row + 64, lanes] = dens_re.astype(bf16)
-                    dens[row : row + 64, lanes_im] = dens_im.astype(bf16)
-
-    densities(0, dens_even)
+                    part = funcs_ref[pl.ds(piece * BLOCKS, BLOCKS), slot]
+                    parts.append(part.astype(f32).reshape(8, 128))
+                return jnp.concatenate(parts, axis=1)
+
+            right_re, right_im = bands(0, 2), bands(1, 2)
+            for pair in range(2):
+                place = (kind * 2 + pair) * 16
+                left[place : place + 8] = bands(0, pair)
+                left[place + 8 : place + 16] = bands(1, pair)
+                for v in range(8):
+                    left_re = left[pl.ds(place + v, 8, stride=0)]
+                    left_im = left[pl.ds(place + 8 + v, 8, stride=0)]
+                    row = (kind * 2 + pair) * 64 + 8 * v
+                    dens_re = left_re * right_re + left_im * right_im
+                    dens_im = left_re * right_im - left_im * right_re
+                    dens[row : row + 8, :PLANE] = dens_re.astype(bf16)
+                    dens[row : row + 8, PLANE:] = dens_im.astype(bf16)
+
+    densities(0, dens_even, left_even)
 
     def planes(i, carry):
         x = 2 * i
         sums[x] = jnp.dot(dens_even[...], table_ref[...], preferred_element_type=f32)
-        densities(x + 1, dens_odd)
+        densities(x + 1, dens_odd, left_odd)
         sums[x + 1] = jnp.dot(dens_odd[...], table_ref[...], preferred_element_type=f32)
-        densities(jnp.minimum(x + 2, SIDE - 1), dens_even)
+        densities(jnp.minimum(x + 2, SIDE - 1), dens_even, left_even)
         return carry
 
     lax.fori_loop(0, SIDE // 2, planes, 0)
@@ -193,58 +200,58 @@
 
     row, lane = iota((64, 128), 0), iota((64, 128), 1)
     row_hi, row_lo = row >> 3, row & 7
-    q, l = iota((128, 64), 0), iota((128, 64), 1)
-    pick_hi = jnp.where((q < 64) & ((q >> 3) == (l >> 3)), 1.0, 0.0).astype(bf16)
-    pick_lo = jnp.where((q < 64) & ((q >> 3) == (l & 7)), 1.0, 0.0).astype(bf16)
-
-    def spread(point, row_band, pick):
-        parts = []
+    q, l = iota((128, 128), 0), iota((128, 128), 1)
+    pick_hi = jnp.where((q >> 3) == ((l >> 3) & 7), 1.0, 0.0).astype(bf16)
+    pick_lo = jnp.where((q >> 3) == (l & 7), 1.0, 0.0).astype(bf16)
+
+    def rows_of(point, row_band):
+        kept = []
         for ri in range(2):
-            values = held_ref[point, 2 + ri : 3 + ri].astype(f32)
-            kept = jnp.where((lane & 7) == row_band, jnp.broadcast_to(values, (64, 128)), 0.0)
-            parts.append(jnp.dot(kept.astype(bf16), pick, preferred_element_type=f32))
-        return parts
-
-    out_band = 2 * (lane >> 5) + ((lane >> 3) & 1)
-    out_part = (lane >> 4) & 1
-    out_other = lane & 7
-    gather_hi = jnp.where(row_hi == out_band, 1.0, 0.0)
-    gather_lo = jnp.where(row_lo == out_band, 1.0, 0.0)
-
-    def collect(re, im, gather, row_band):
-        dot = functools.partial(
-            jnp.dot, precision=lax.Precision.HIGHEST, preferred_element_type=f32
-        )
-        both = dot(re, jnp.where(out_part == 0, gather, 0.0)) + dot(
-            im, jnp.where(out_part == 1, gather, 0.0)
-        )
-        return jnp.sum(jnp.where(row_band == out_other, both, 0.0), axis=0, keepdims=True)
-
-    far_re, far_im = spread(move, row_lo, pick_lo)
+            values = jnp.broadcast_to(held_ref[point, 2 + ri : 3 + ri].astype(f32), (64, 128))
+            kept.append(jnp.where((lane & 7) == row_band, values, 0.0))
+        return kept
+
+    def spread(kept, pick):
+        kept = jnp.concatenate(kept, axis=0).astype(bf16)
+        return jnp.dot(kept, pick, preferred_element_type=f32)
+
+    far = spread(rows_of(move, row_lo), pick_lo)
+    near = spread(rows_of(first_point[0], row_hi) + rows_of(first_point[1], row_hi), pick_hi)
+    minus_low = jnp.where(lane < 64, -1.0, 1.0)
+    far_re, far_im = far[:64], far[64:] * minus_low
+
+    out_band = 2 * (l >> 5) + ((l >> 3) & 1)
+    out_part = (l >> 4) & 1
+    part = (q >> 6) == out_part
+    gather_hi = jnp.where(part & (((q >> 3) & 7) == out_band), 1.0, 0.0).astype(bf16)
+    gather_lo = jnp.where(part & ((q & 7) == out_band), 1.0, 0.0).astype(bf16)
+
+    def collect(values, gather, row_band):
+        high = values.astype(bf16)
+        rest = values - high.astype(f32)
+        middle = rest.astype(bf16)
+        low = (rest - middle.astype(f32)).astype(bf16)
+        both = sum(jnp.dot(p, gather, preferred_element_type=f32) for p in (high, middle, low))
+        return jnp.sum(jnp.where(row_band == (lane & 7), both, 0.0), axis=0, keepdims=True)
+
     r = iota((points, 128), 0)
     k = ((r & 7) << 4) | (r >> 3)
     total = jnp.zeros((points, 128), f32)
-    back_re = back_im = 0.0
+    back = 0.0
     for pair, weights in enumerate((own_ref, other_ref)):
         val, cond = slice(64 * pair, 64 * pair + 64), slice(128 + 64 * pair, 192 + 64 * pair)
         stacked = jnp.concatenate([wave_re[val], wave_im[val]], axis=0)
         with_re, with_im = nt(stacked, weights[0]), nt(stacked, weights[1])
-        scr_re = (with_re[:64] - with_im[64:]).astype(bf16)
-        scr_im = (with_re[64:] + with_im[:64]).astype(bf16)
-        cond_re, cond_im = wave_re[cond], wave_im[cond]
-        kern_re = (nt(cond_re, scr_re) + nt(cond_im, scr_im)) * (1.0 / NG)
-        kern_im = (nt(cond_re, scr_im) - nt(cond_im, scr_re)) * (1.0 / NG)
-        near_re, near_im = spread(first_point[pair], row_hi, pick_hi)
-        direct = collect(
-            kern_re * far_re - kern_im * far_im,
-            kern_re * far_im + kern_im * far_re,
-            gather_hi,
-            row_hi,
-        )
-        back_re += kern_re * near_re + kern_im * near_im
-        back_im += kern_re * near_im - kern_im * near_re
+        scr_re, scr_im = with_re[:64] - with_im[64:], with_re[64:] + with_im[:64]
+        straight = jnp.concatenate([scr_re, scr_im], axis=0).astype(bf16)
+        turned = jnp.concatenate([scr_im, -scr_re], axis=0).astype(bf16)
+        kern = (nt(wave_re[cond], straight) + nt(wave_im[cond], turned)) * (1.0 / NG)
+        swapped = pltpu.roll(kern, 64, 1)
+        near_re, near_im = near[128 * pair : 128 * pair + 64], near[128 * pair + 64 : 128 * pair + 128]
+        direct = collect(kern * far_re + swapped * far_im, gather_hi, row_hi)
+        back += swapped * near_im - kern * (near_re * minus_low)
         total += jnp.where(k == first_point[pair], jnp.broadcast_to(direct, (points, 128)), 0.0)
-    back = collect(back_re, back_im, gather_lo, row_lo)
+    back = collect(back, gather_lo, row_lo)
     total += jnp.where(k == move, jnp.broadcast_to(back, (points, 128)), 0.0)
     out_ref[...] = total
 
@@ -260,6 +267,8 @@
         scratch_shapes=[
             pltpu.VMEM((256, 2 * PLANE), jnp.bfloat16),
             pltpu.VMEM((256, 2 * PLANE), jnp.bfloat16),
+            pltpu.VMEM((72, PLANE), jnp.float32),
+            pltpu.VMEM((72, PLANE), jnp.float32),
             pltpu.VMEM((SIDE, 256, 4 * HALF), jnp.float32),
             pltpu.VMEM((256, NG), jnp.bfloat16),
             pltpu.VMEM((256, NG), jnp.bfloat16),

time: 105 us -> 104 us (level)
  local copies, waits for them, and re-layouts: 2.32 us -> 0.83 us
    unnamed x11 -> x7, local copies, waits for them, and re-layouts: 1.59 us -> 0.09 us
where the time goes in v4:
time: 104 us
  starting transfers between devices  34.2 us (33%)
  waiting for transfers between devices  33.2 us (32%)
  blocking collectives  24.2 us (23%)
  Pallas kernels  11.3 us (11%)
    all_to_all x1, waiting for transfers between devices, local(): lax.all_to_all(send_pieces(pair_list, held), ('kq', 'band'), 0, 0, tiled=...  18.9 us
    all_to_all x1, starting transfers between devices, local(): held = lax.all_to_all(pack_pieces(pieces, exciton), 'kq', 0, 0, tiled=True)  18.5 us
    all_to_all x1, blocking collectives, local(): lax.all_to_all(parts, ('kq', 'band'), 0, 0, tiled=True, axis_index_groups...  12.3 us
    all_to_all x1, waiting for transfers between devices, local(): held = lax.all_to_all(pack_pieces(pieces, exciton), 'kq', 0, 0, tiled=True)  12.2 us
    all_to_all x1, blocking collectives, local(): lax.all_to_all(terms.reshape(16, 8, 128), 'kq', 0, 0, tiled=True, axis_in...  11.9 us
    all_to_all x1, starting transfers between devices, local(): lax.all_to_all(send_pieces(pair_list, held), ('kq', 'band'), 0, 0, tiled=...  9.31 us
    pallas_call x1, Pallas kernels, pair_terms(): pl.pallas_call(pair_body, out_shape=jax.ShapeDtypeStruct((points, 128), j...  7.46 us
    ppermute x1, starting transfers between devices, local(): other = lax.ppermute(screening, 'kq', [(i, i ^ 1) for i in range(points)])  6.35 us
  transfers between devices with their start and end apart: 3, of which 3 were waited for; matrix products, arithmetic and copies ran while one was open for 0% of the time, Pallas kernels for 0%

profile of v4, /device:TPU:1, one launch (start us, length us, event | category | flops | bytes accessed | tf_op | source)
XLA Modules:
  0.0 104.0 jit_solution(14595878851202021088)
XLA Ops:
  0.0 1.6 %pack_pieces.1 = bf16[128,4,128]{2,1,0:T(4,128)(2,1)} custom-call(bf16[128,2,128]{2,1,0:T(2,128)(2,1)} %bitcast.13, bf16[1,2,64]{2,1,0:T(2,128)(2,1)} %exciton_ref.1), custom_call_target="tpu_custom_call" | custom-call | tf_op jit(solution)/shard_map/pack_pieces/pallas_call | solution.py:62
  1.6 0.0 copy-start.2
  1.6 18.5 %all-to-all-start = ((bf16[128,4,128]{2,1,0:T(4,128)(2,1)}), bf16[128,4,128]{2,1,0:T(4,128)(2,1)S(1)}, u32[]{:S(2)}, u32[]{:S(2)}) async-start(bf16[128,4,128]{2,1,0:T(4,128)(2,1)} %pack_pieces.1), calls=%async_computation | async-start | bytes 262144 | tf_op jit(solution)/shard_map/all_to_all | solution.py:290
  20.1 0.0 copy-done.2
  20.1 0.1 copy.11.pairs_ref
  20.2 0.0 copy-start
  20.2 12.2 %all-to-all-done.held_ref = bf16[128,4,128]{2,1,0:T(4,128)(2,1)S(1)} async-done(((bf16[128,4,128]{2,1,0:T(4,128)(2,1)}), bf16[128,4,128]{2,1,0:T(4,128)(2,1)S(1)}, u32[]{:S(2)}, u32[]{:S(2)}) %all-to-all-start) | async-done | bytes 131104 | tf_op jit(solution)/shard_map/all_to_all | solution.py:290
  32.4 2.3 %send_pieces.1 = bf16[512,3,2,128]{3,2,1,0:T(2,128)(2,1)} custom-call(s32[8,2]{1,0:T(8,128)S(1)} %copy.11.pairs_ref, bf16[128,4,128]{2,1,0:T(4,128)(2,1)S(1)} %all-to-all-done.held_ref), custom_call_target="tpu_custom_call" | custom-call | tf_op jit(solution)/shard_map/send_pieces/pallas_call | solution.py:95
  34.7 0.0 copy-start.1
  34.7 9.3 %all-to-all-start.1 = ((bf16[512,3,2,128]{3,2,1,0:T(2,128)(2,1)}), bf16[512,3,2,128]{3,2,1,0:T(2,128)(2,1)S(1)}, u32[]{:S(2)}, u32[]{:S(2)}) async-start(bf16[512,3,2,128]{3,2,1,0:T(2,128)(2,1)} %send_pieces.1), calls=%async_computation.1 | async-start | bytes 1572864 | tf_op jit(solution)/shard_map/all_to_all | solution.py:292
  44.0 0.0 copy-done
  44.0 6.3 %collective-permute-start = (bf16[1,2,512,512]{3,2,1,0:T(8,128)(2,1)S(1)}, bf16[1,2,512,512]{3,2,1,0:T(8,128)(2,1)S(1)}, u32[]{:S(2)}, u32[]{:S(2)}) collective-permute-start(bf16[1,2,512,512]{3,2,1,0:T(8,128)(2,1)S(1)} %copy-done), channel_id=1, source_target_pairs={{0,4},{4,0},{8,12},{12,8},{16,20},{20,16},{24,28},{28,24},{32,36},... | collective-permute-start | bytes 3145736 | tf_op jit(solution)/shard_map/ppermute | solution.py:287
  50.3 0.1 pad_add_fusion.place_ref
  50.4 2.2 %collective-permute-done = bf16[1,2,512,512]{3,2,1,0:T(8,128)(2,1)S(1)} collective-permute-done((bf16[1,2,512,512]{3,2,1,0:T(8,128)(2,1)S(1)}, bf16[1,2,512,512]{3,2,1,0:T(8,128)(2,1)S(1)}, u32[]{:S(2)}, u32[]{:S(2)}) %collective-permute-start) | collective-permute-done | bytes 1048608 | tf_op jit(solution)/shard_map/ppermute | solution.py:287
  52.6 18.9 %all-to-all-done.1.funcs_ref = bf16[512,3,2,128]{3,2,1,0:T(2,128)(2,1)S(1)} async-done(((bf16[512,3,2,128]{3,2,1,0:T(2,128)(2,1)}), bf16[512,3,2,128]{3,2,1,0:T(2,128)(2,1)S(1)}, u32[]{:S(2)}, u32[]{:S(2)}) %all-to-all-start.1) | async-done | bytes 786464 | tf_op jit(solution)/shard_map/all_to_all | solution.py:292
  71.5 0.0 copy-done.1
  71.5 7.5 %pair_terms.1 = f32[128,128]{1,0:T(8,128)S(1)} custom-call(s32[2]{0:T(128)S(1)} %pad_add_fusion.place_ref, s32[8,2]{1,0:T(8,128)S(1)} %copy.11.pairs_ref, bf16[512,3,2,128]{3,2,1,0:T(2,128)(2,1)S(1)} %all-to-all-done.1.funcs_ref, bf16[2,512,512]{2,1,0:T(8,128)(2,1)S(1)} %bitcast.10, bf16[2,512,512]{2,1,0:T(8,128)(2,1)S(1)} %bitcast.11, ...), custom_call_target="tpu_custom_call" | custom-call | tf_op jit(solution)/shard_map/pair_terms/pallas_call | solution.py:262
  79.0 11.9 %all_to_all.20 = f32[16,8,128]{2,1,0:T(8,128)S(1)} all-to-all(f32[16,8,128]{2,1,0:T(8,128)S(1)} %bitcast.12), channel_id=1, replica_groups={{0,4,8,12,16,20,24,28,32,36,40,44,48,52,56,60},{64,68,72,76,80,84,88,92..., dimensions={0} | all-to-all | bytes 131072 | tf_op jit(solution)/shard_map/all_to_all | solution.py:299
  90.9 0.1 reshape.18
  91.0 12.3 %all_to_all.21 = f32[32,1,32]{2,1,0:T(1,128)S(1)} all-to-all(f32[32,1,32]{2,1,0:T(1,128)S(1)} %reshape.18), channel_id=1, replica_groups={{0,1,2,3,64,65,66,67,128,129,130,131,192,193,194,195,256,257,258,259,32..., dimensions={0} | all-to-all | bytes 8192 | tf_op jit(solution)/shard_map/all_to_all | solution.py:303
  103.3 0.1 reduce_sum.19
  103.3 0.6 reshape.19
  (1 shorter events, 0.0 us)
Async XLA Ops:
  1.6 18.6 %copy-start.2 = (s32[8,2]{0,1:T(2,128)S(1)}, s32[8,2]{0,1:T(2,128)}, u32[]{:S(2)}) copy-start(s32[8,2]{0,1:T(2,128)} %param.8) | copy-start | bytes 196
  1.6 30.8 %all-to-all-start = ((bf16[128,4,128]{2,1,0:T(4,128)(2,1)}), bf16[128,4,128]{2,1,0:T(4,128)(2,1)S(1)}, u32[]{:S(2)}, u32[]{:S(2)}) async-start(bf16[128,4,128]{2,1,0:T(4,128)(2,1)} %pack_pieces.1), calls=%async_computation | async-start | bytes 262144 | tf_op jit(solution)/shard_map/all_to_all | solution.py:290
  20.2 23.8 %copy-start = (bf16[1,2,512,512]{3,2,1,0:T(8,128)(2,1)S(1)}, bf16[1,2,512,512]{3,2,1,0:T(8,128)(2,1)}, u32[]{:S(2)}) copy-start(bf16[1,2,512,512]{3,2,1,0:T(8,128)(2,1)} %param.6) | copy-start | bytes 3145732
  34.7 36.8 %copy-start.1 = (bf16[512,256]{1,0:T(8,128)(2,1)S(1)}, bf16[512,256]{1,0:T(8,128)(2,1)}, u32[]{:S(2)}) copy-start(bf16[512,256]{1,0:T(8,128)(2,1)} %constant.13.clone.table_ref) | copy-start | bytes 786436
  34.7 36.8 %all-to-all-start.1 = ((bf16[512,3,2,128]{3,2,1,0:T(2,128)(2,1)}), bf16[512,3,2,128]{3,2,1,0:T(2,128)(2,1)S(1)}, u32[]{:S(2)}, u32[]{:S(2)}) async-start(bf16[512,3,2,128]{3,2,1,0:T(2,128)(2,1)} %send_pieces.1), calls=%async_computation.1 | async-start | bytes 1572864 | tf_op jit(solution)/shard_map/all_to_all | solution.py:292
  44.0 8.6 %collective-permute-start = (bf16[1,2,512,512]{3,2,1,0:T(8,128)(2,1)S(1)}, bf16[1,2,512,512]{3,2,1,0:T(8,128)(2,1)S(1)}, u32[]{:S(2)}, u32[]{:S(2)}) collective-permute-start(bf16[1,2,512,512]{3,2,1,0:T(8,128)(2,1)S(1)} %copy-done), channel_id=1, source_target_pairs={{0,4},{4,0},{8,12},{12,8},{16,20},{20,16},{24,28},{28,24},{32,36},... | collective-permute-start | bytes 3145736 | tf_op jit(solution)/shard_map/ppermute | solution.py:287

commit v5 on v4

--- a/solution.py
+++ b/solution.py
@@ -15,6 +15,8 @@
 HALF = BOX * BOX
 NG = BOX * HALF
 BLOCKS = 4
+QUARTERS = 4
+AT_ONCE = 2
 NT = (((1,), (1,)), ((), ()))
 
 
@@ -69,8 +71,9 @@
     )(pieces, exciton)
 
 
-def send_body(pairs_ref, held_ref, sent_ref, twice):
+def send_body(pairs_ref, held_ref, sent_ref, twice, built, done):
     points = held_ref.shape[0]
+    part = built.shape[0] // QUARTERS
     twice[0:points] = held_ref[...]
     twice[points : 2 * points] = held_ref[...]
     moves = [[second_of(pairs_ref, block, parity) for block in range(BLOCKS)] for parity in range(2)]
@@ -81,23 +84,38 @@
             for block in range(BLOCKS):
                 target = (2 * i + parity) * BLOCKS + block
                 run = 2 * i + moves[parity][block]
-                sent_ref[target, 0] = twice[run + parity, 0:2]
-                sent_ref[target, 1] = twice[run + (1 - parity), 0:2]
-                sent_ref[target, 2] = right[parity][block]
+                built[target, 0] = twice[run + parity, 0:2]
+                built[target, 1] = twice[run + (1 - parity), 0:2]
+                built[target, 2] = right[parity][block]
         return carry
 
-    lax.fori_loop(0, points // 2, chip, 0, unroll=2)
+    copies = []
+    chips = points // (2 * QUARTERS)
+    for quarter in range(QUARTERS):
+        lax.fori_loop(quarter * chips, (quarter + 1) * chips, chip, 0, unroll=2)
+        rows = pl.ds(quarter * part, part)
+        copies.append(pltpu.make_async_copy(built.at[rows], sent_ref.at[rows], done.at[quarter]))
+        copies[-1].start()
+    for copy in copies:
+        copy.wait()
 
 
 def send_pieces(pairs, held, interpret=False):
     points = held.shape[0]
-    vmem = pl.BlockSpec(memory_space=pltpu.VMEM)
+    shape = (points * BLOCKS, 3, 2, 128)
     return pl.pallas_call(
         send_body,
-        out_shape=jax.ShapeDtypeStruct((points * BLOCKS, 3, 2, 128), jnp.bfloat16),
-        in_specs=[pl.BlockSpec(memory_space=pltpu.SMEM), vmem],
-        out_specs=vmem,
-        scratch_shapes=[pltpu.VMEM((2 * points, 4, 128), jnp.bfloat16)],
+        out_shape=jax.ShapeDtypeStruct(shape, jnp.bfloat16),
+        in_specs=[
+            pl.BlockSpec(memory_space=pltpu.SMEM),
+            pl.BlockSpec(memory_space=pltpu.VMEM),
+        ],
+        out_specs=pl.BlockSpec(memory_space=pl.ANY),
+        scratch_shapes=[
+            pltpu.VMEM((2 * points, 4, 128), jnp.bfloat16),
+            pltpu.VMEM(shape, jnp.bfloat16),
+            pltpu.SemaphoreType.DMA((QUARTERS,)),
+        ],
         compiler_params=pltpu.CompilerParams(vmem_limit_bytes=4 << 20),
         name="send_pieces",
         interpret=interpret,
@@ -149,17 +167,26 @@
                     dens[row : row + 8, :PLANE] = dens_re.astype(bf16)
                     dens[row : row + 8, PLANE:] = dens_im.astype(bf16)
 
-    densities(0, dens_even, left_even)
+    def fill(x, dens, left):
+        for i in range(AT_ONCE):
+            densities(x + i, dens.at[pl.ds(256 * i, 256)], left)
+
+    def sum_up(x, dens):
+        both = jnp.dot(dens[...], table_ref[...], preferred_element_type=f32)
+        for i in range(AT_ONCE):
+            sums[x + i] = both[256 * i : 256 * i + 256]
+
+    fill(0, dens_even, left_even)
 
     def planes(i, carry):
-        x = 2 * i
-        sums[x] = jnp.dot(dens_even[...], table_ref[...], preferred_element_type=f32)
-        densities(x + 1, dens_odd, left_odd)
-        sums[x + 1] = jnp.dot(dens_odd[...], table_ref[...], preferred_element_type=f32)
-        densities(jnp.minimum(x + 2, SIDE - 1), dens_even, left_even)
+        x = 2 * AT_ONCE * i
+        sum_up(x, dens_even)
+        fill(x + AT_ONCE, dens_odd, left_odd)
+        sum_up(x + AT_ONCE, dens_odd)
+        fill(jnp.minimum(x + 2 * AT_ONCE, SIDE - AT_ONCE), dens_even, left_even)
         return carry
 
-    lax.fori_loop(0, SIDE // 2, planes, 0)
+    lax.fori_loop(0, SIDE // (2 * AT_ONCE), planes, 0)
 
     scale = 1.0 / math.sqrt(SIDE**3)
     low_lanes = iota((16, 128), 1) < HALF
@@ -265,8 +292,8 @@
         in_specs=[smem, smem] + [vmem] * 5,
         out_specs=vmem,
         scratch_shapes=[
-            pltpu.VMEM((256, 2 * PLANE), jnp.bfloat16),
-            pltpu.VMEM((256, 2 * PLANE), jnp.bfloat16),
+            pltpu.VMEM((AT_ONCE * 256, 2 * PLANE), jnp.bfloat16),
+            pltpu.VMEM((AT_ONCE * 256, 2 * PLANE), jnp.bfloat16),
             pltpu.VMEM((72, PLANE), jnp.float32),
             pltpu.VMEM((72, PLANE), jnp.float32),
             pltpu.VMEM((SIDE, 256, 4 * HALF), jnp.float32),

time: 104 us -> 103 us (level)
  no operation moved by 1% of the time
where the time goes in v5:
time: 103 us
  starting transfers between devices  34.2 us (33%)
  waiting for transfers between devices  33.2 us (32%)
  blocking collectives  24.2 us (23%)
  Pallas kernels  10.4 us (10%)
    all_to_all x1, waiting for transfers between devices, local(): lax.all_to_all(send_pieces(pair_list, held), ('kq', 'band'), 0, 0, tiled=...  18.9 us
    all_to_all x1, starting transfers between devices, local(): held = lax.all_to_all(pack_pieces(pieces, exciton), 'kq', 0, 0, tiled=True)  18.5 us
    all_to_all x1, blocking collectives, local(): lax.all_to_all(parts, ('kq', 'band'), 0, 0, tiled=True, axis_index_groups...  12.3 us
    all_to_all x1, waiting for transfers between devices, local(): held = lax.all_to_all(pack_pieces(pieces, exciton), 'kq', 0, 0, tiled=True)  12.2 us
    all_to_all x1, blocking collectives, local(): lax.all_to_all(terms.reshape(16, 8, 128), 'kq', 0, 0, tiled=True, axis_in...  11.9 us
    all_to_all x1, starting transfers between devices, local(): lax.all_to_all(send_pieces(pair_list, held), ('kq', 'band'), 0, 0, tiled=...  9.33 us
    pallas_call x1, Pallas kernels, pair_terms(): pl.pallas_call(pair_body, out_shape=jax.ShapeDtypeStruct((points, 128), j...  6.79 us
    ppermute x1, starting transfers between devices, local(): other = lax.ppermute(screening, 'kq', [(i, i ^ 1) for i in range(points)])  6.35 us
  transfers between devices with their start and end apart: 3, of which 3 were waited for; matrix products, arithmetic and copies ran while one was open for 0% of the time, Pallas kernels for 0%

profile of v5, /device:TPU:1, one launch (start us, length us, event | category | flops | bytes accessed | tf_op | source)
XLA Modules:
  0.0 103.1 jit_solution(3893050388970052630)
XLA Ops:
  0.0 1.6 %pack_pieces.1 = bf16[128,4,128]{2,1,0:T(4,128)(2,1)} custom-call(bf16[128,2,128]{2,1,0:T(2,128)(2,1)} %bitcast.13, bf16[1,2,64]{2,1,0:T(2,128)(2,1)} %exciton_ref.1), custom_call_target="tpu_custom_call" | custom-call | tf_op jit(solution)/shard_map/pack_pieces/pallas_call | solution.py:64
  1.6 0.0 copy-start.2
  1.6 18.5 %all-to-all-start = ((bf16[128,4,128]{2,1,0:T(4,128)(2,1)}), bf16[128,4,128]{2,1,0:T(4,128)(2,1)S(1)}, u32[]{:S(2)}, u32[]{:S(2)}) async-start(bf16[128,4,128]{2,1,0:T(4,128)(2,1)} %pack_pieces.1), calls=%async_computation | async-start | bytes 262144 | tf_op jit(solution)/shard_map/all_to_all | solution.py:317
  20.1 0.0 copy-done.2
  20.1 0.1 copy.11.pairs_ref
  20.2 0.0 copy-start
  20.2 12.2 %all-to-all-done.held_ref = bf16[128,4,128]{2,1,0:T(4,128)(2,1)S(1)} async-done(((bf16[128,4,128]{2,1,0:T(4,128)(2,1)}), bf16[128,4,128]{2,1,0:T(4,128)(2,1)S(1)}, u32[]{:S(2)}, u32[]{:S(2)}) %all-to-all-start) | async-done | bytes 131104 | tf_op jit(solution)/shard_map/all_to_all | solution.py:317
  32.4 2.1 %send_pieces.1 = bf16[512,3,2,128]{3,2,1,0:T(2,128)(2,1)} custom-call(s32[8,2]{1,0:T(8,128)S(1)} %copy.11.pairs_ref, bf16[128,4,128]{2,1,0:T(4,128)(2,1)S(1)} %all-to-all-done.held_ref), custom_call_target="tpu_custom_call" | custom-call | tf_op jit(solution)/shard_map/send_pieces/pallas_call | solution.py:106
  34.5 0.0 copy-start.1
  34.5 9.3 %all-to-all-start.1 = ((bf16[512,3,2,128]{3,2,1,0:T(2,128)(2,1)}), bf16[512,3,2,128]{3,2,1,0:T(2,128)(2,1)S(1)}, u32[]{:S(2)}, u32[]{:S(2)}) async-start(bf16[512,3,2,128]{3,2,1,0:T(2,128)(2,1)} %send_pieces.1), calls=%async_computation.1 | async-start | bytes 1572864 | tf_op jit(solution)/shard_map/all_to_all | solution.py:319
  43.8 0.0 copy-done
  43.8 6.3 %collective-permute-start = (bf16[1,2,512,512]{3,2,1,0:T(8,128)(2,1)S(1)}, bf16[1,2,512,512]{3,2,1,0:T(8,128)(2,1)S(1)}, u32[]{:S(2)}, u32[]{:S(2)}) collective-permute-start(bf16[1,2,512,512]{3,2,1,0:T(8,128)(2,1)S(1)} %copy-done), channel_id=1, source_target_pairs={{0,4},{4,0},{8,12},{12,8},{16,20},{20,16},{24,28},{28,24},{32,36},... | collective-permute-start | bytes 3145736 | tf_op jit(solution)/shard_map/ppermute | solution.py:314
  50.2 0.1 pad_add_fusion.place_ref
  50.3 2.2 %collective-permute-done = bf16[1,2,512,512]{3,2,1,0:T(8,128)(2,1)S(1)} collective-permute-done((bf16[1,2,512,512]{3,2,1,0:T(8,128)(2,1)S(1)}, bf16[1,2,512,512]{3,2,1,0:T(8,128)(2,1)S(1)}, u32[]{:S(2)}, u32[]{:S(2)}) %collective-permute-start) | collective-permute-done | bytes 1048608 | tf_op jit(solution)/shard_map/ppermute | solution.py:314
  52.4 18.9 %all-to-all-done.1.funcs_ref = bf16[512,3,2,128]{3,2,1,0:T(2,128)(2,1)S(1)} async-done(((bf16[512,3,2,128]{3,2,1,0:T(2,128)(2,1)}), bf16[512,3,2,128]{3,2,1,0:T(2,128)(2,1)S(1)}, u32[]{:S(2)}, u32[]{:S(2)}) %all-to-all-start.1) | async-done | bytes 786464 | tf_op jit(solution)/shard_map/all_to_all | solution.py:319
  71.3 0.0 copy-done.1
  71.3 6.8 %pair_terms.1 = f32[128,128]{1,0:T(8,128)S(1)} custom-call(s32[2]{0:T(128)S(1)} %pad_add_fusion.place_ref, s32[8,2]{1,0:T(8,128)S(1)} %copy.11.pairs_ref, bf16[512,3,2,128]{3,2,1,0:T(2,128)(2,1)S(1)} %all-to-all-done.1.funcs_ref, bf16[2,512,512]{2,1,0:T(8,128)(2,1)S(1)} %bitcast.10, bf16[2,512,512]{2,1,0:T(8,128)(2,1)S(1)} %bitcast.11, ...), custom_call_target="tpu_custom_call" | custom-call | tf_op jit(solution)/shard_map/pair_terms/pallas_call | solution.py:289
  78.1 11.9 %all_to_all.20 = f32[16,8,128]{2,1,0:T(8,128)S(1)} all-to-all(f32[16,8,128]{2,1,0:T(8,128)S(1)} %bitcast.12), channel_id=1, replica_groups={{0,4,8,12,16,20,24,28,32,36,40,44,48,52,56,60},{64,68,72,76,80,84,88,92..., dimensions={0} | all-to-all | bytes 131072 | tf_op jit(solution)/shard_map/all_to_all | solution.py:326
  90.0 0.1 reshape.18
  90.1 12.3 %all_to_all.21 = f32[32,1,32]{2,1,0:T(1,128)S(1)} all-to-all(f32[32,1,32]{2,1,0:T(1,128)S(1)} %reshape.18), channel_id=1, replica_groups={{0,1,2,3,64,65,66,67,128,129,130,131,192,193,194,195,256,257,258,259,32..., dimensions={0} | all-to-all | bytes 8192 | tf_op jit(solution)/shard_map/all_to_all | solution.py:330
  102.4 0.1 reduce_sum.19
  102.5 0.6 reshape.19
  (1 shorter events, 0.0 us)
Async XLA Ops:
  1.6 18.6 %copy-start.2 = (s32[8,2]{0,1:T(2,128)S(1)}, s32[8,2]{0,1:T(2,128)}, u32[]{:S(2)}) copy-start(s32[8,2]{0,1:T(2,128)} %param.8) | copy-start | bytes 196
  1.6 30.8 %all-to-all-start = ((bf16[128,4,128]{2,1,0:T(4,128)(2,1)}), bf16[128,4,128]{2,1,0:T(4,128)(2,1)S(1)}, u32[]{:S(2)}, u32[]{:S(2)}) async-start(bf16[128,4,128]{2,1,0:T(4,128)(2,1)} %pack_pieces.1), calls=%async_computation | async-start | bytes 262144 | tf_op jit(solution)/shard_map/all_to_all | solution.py:317
  20.2 23.6 %copy-start = (bf16[1,2,512,512]{3,2,1,0:T(8,128)(2,1)S(1)}, bf16[1,2,512,512]{3,2,1,0:T(8,128)(2,1)}, u32[]{:S(2)}) copy-start(bf16[1,2,512,512]{3,2,1,0:T(8,128)(2,1)} %param.6) | copy-start | bytes 3145732
  34.5 36.9 %copy-start.1 = (bf16[512,256]{1,0:T(8,128)(2,1)S(1)}, bf16[512,256]{1,0:T(8,128)(2,1)}, u32[]{:S(2)}) copy-start(bf16[512,256]{1,0:T(8,128)(2,1)} %constant.13.clone.table_ref) | copy-start | bytes 786436
  34.5 36.8 %all-to-all-start.1 = ((bf16[512,3,2,128]{3,2,1,0:T(2,128)(2,1)}), bf16[512,3,2,128]{3,2,1,0:T(2,128)(2,1)S(1)}, u32[]{:S(2)}, u32[]{:S(2)}) async-start(bf16[512,3,2,128]{3,2,1,0:T(2,128)(2,1)} %send_pieces.1), calls=%async_computation.1 | async-start | bytes 1572864 | tf_op jit(solution)/shard_map/all_to_all | solution.py:319
  43.8 8.6 %collective-permute-start = (bf16[1,2,512,512]{3,2,1,0:T(8,128)(2,1)S(1)}, bf16[1,2,512,512]{3,2,1,0:T(8,128)(2,1)S(1)}, u32[]{:S(2)}, u32[]{:S(2)}) collective-permute-start(bf16[1,2,512,512]{3,2,1,0:T(8,128)(2,1)S(1)} %copy-done), channel_id=1, source_target_pairs={{0,4},{4,0},{8,12},{12,8},{16,20},{20,16},{24,28},{28,24},{32,36},... | collective-permute-start | bytes 3145736 | tf_op jit(solution)/shard_map/ppermute | solution.py:314

commit v6 on v5

--- a/solution.py
+++ b/solution.py
@@ -92,7 +92,7 @@
     copies = []
     chips = points // (2 * QUARTERS)
     for quarter in range(QUARTERS):
-        lax.fori_loop(quarter * chips, (quarter + 1) * chips, chip, 0, unroll=2)
+        lax.fori_loop(quarter * chips, (quarter + 1) * chips, chip, 0, unroll=8)
         rows = pl.ds(quarter * part, part)
         copies.append(pltpu.make_async_copy(built.at[rows], sent_ref.at[rows], done.at[quarter]))
         copies[-1].start()
@@ -186,7 +186,7 @@
         fill(jnp.minimum(x + 2 * AT_ONCE, SIDE - AT_ONCE), dens_even, left_even)
         return carry
 
-    lax.fori_loop(0, SIDE // (2 * AT_ONCE), planes, 0)
+    lax.fori_loop(0, SIDE // (2 * AT_ONCE), planes, 0, unroll=2)
 
     scale = 1.0 / math.sqrt(SIDE**3)
     low_lanes = iota((16, 128), 1) < HALF
@@ -216,7 +216,7 @@
             wave_im[rows, pair * 128 : pair * 128 + 128] = im.astype(bf16)
         return carry
 
-    lax.fori_loop(0, 16, along_x, 0)
+    lax.fori_loop(0, 16, along_x, 0, unroll=16)
 
     def nt(a, b):
         return lax.dot_general(a, b, NT, preferred_element_type=f32)

time: 103 us -> 101 us (0.981)
  Pallas kernels: 10.4 us -> 8.42 us
    pallas_call x1, Pallas kernels: 6.79 us -> 4.98 us  [pair_terms(): pl.pallas_call(pair_body, out_shape=jax.ShapeDtypeStruct((points, 128), j...]
where the time goes in v6:
time: 101 us
  starting transfers between devices  34.2 us (34%)
  waiting for transfers between devices  33.2 us (33%)
  blocking collectives  24.2 us (24%)
  Pallas kernels  8.42 us (8%)
    all_to_all x1, waiting for transfers between devices, local(): lax.all_to_all(send_pieces(pair_list, held), ('kq', 'band'), 0, 0, tiled=...  18.9 us
    all_to_all x1, starting transfers between devices, local(): held = lax.all_to_all(pack_pieces(pieces, exciton), 'kq', 0, 0, tiled=True)  18.5 us
    all_to_all x1, blocking collectives, local(): lax.all_to_all(parts, ('kq', 'band'), 0, 0, tiled=True, axis_index_groups...  12.4 us
    all_to_all x1, waiting for transfers between devices, local(): held = lax.all_to_all(pack_pieces(pieces, exciton), 'kq', 0, 0, tiled=True)  12.2 us
    all_to_all x1, blocking collectives, local(): lax.all_to_all(terms.reshape(16, 8, 128), 'kq', 0, 0, tiled=True, axis_in...  11.8 us
    all_to_all x1, starting transfers between devices, local(): lax.all_to_all(send_pieces(pair_list, held), ('kq', 'band'), 0, 0, tiled=...  9.33 us
    ppermute x1, starting transfers between devices, local(): other = lax.ppermute(screening, 'kq', [(i, i ^ 1) for i in range(points)])  6.35 us
    pallas_call x1, Pallas kernels, pair_terms(): pl.pallas_call(pair_body, out_shape=jax.ShapeDtypeStruct((points, 128), j...  4.98 us
  transfers between devices with their start and end apart: 3, of which 3 were waited for; matrix products, arithmetic and copies ran while one was open for 0% of the time, Pallas kernels for 0%

profile of v6, /device:TPU:1, one launch (start us, length us, event | category | flops | bytes accessed | tf_op | source)
XLA Modules:
  0.0 101.1 jit_solution(4786998354093303157)
XLA Ops:
  0.0 1.6 %pack_pieces.1 = bf16[128,4,128]{2,1,0:T(4,128)(2,1)} custom-call(bf16[128,2,128]{2,1,0:T(2,128)(2,1)} %bitcast.13, bf16[1,2,64]{2,1,0:T(2,128)(2,1)} %exciton_ref.1), custom_call_target="tpu_custom_call" | custom-call | tf_op jit(solution)/shard_map/pack_pieces/pallas_call | solution.py:64
  1.6 0.0 copy-start.2
  1.6 18.5 %all-to-all-start = ((bf16[128,4,128]{2,1,0:T(4,128)(2,1)}), bf16[128,4,128]{2,1,0:T(4,128)(2,1)S(1)}, u32[]{:S(2)}, u32[]{:S(2)}) async-start(bf16[128,4,128]{2,1,0:T(4,128)(2,1)} %pack_pieces.1), calls=%async_computation | async-start | bytes 262144 | tf_op jit(solution)/shard_map/all_to_all | solution.py:317
  20.1 0.0 copy-done.2
  20.1 0.1 copy.11.pairs_ref
  20.2 0.0 copy-start
  20.2 12.2 %all-to-all-done.held_ref = bf16[128,4,128]{2,1,0:T(4,128)(2,1)S(1)} async-done(((bf16[128,4,128]{2,1,0:T(4,128)(2,1)}), bf16[128,4,128]{2,1,0:T(4,128)(2,1)S(1)}, u32[]{:S(2)}, u32[]{:S(2)}) %all-to-all-start) | async-done | bytes 131104 | tf_op jit(solution)/shard_map/all_to_all | solution.py:317
  32.4 1.9 %send_pieces.1 = bf16[512,3,2,128]{3,2,1,0:T(2,128)(2,1)} custom-call(s32[8,2]{1,0:T(8,128)S(1)} %copy.11.pairs_ref, bf16[128,4,128]{2,1,0:T(4,128)(2,1)S(1)} %all-to-all-done.held_ref), custom_call_target="tpu_custom_call" | custom-call | tf_op jit(solution)/shard_map/send_pieces/pallas_call | solution.py:106
  34.3 0.0 copy-start.1
  34.3 9.3 %all-to-all-start.1 = ((bf16[512,3,2,128]{3,2,1,0:T(2,128)(2,1)}), bf16[512,3,2,128]{3,2,1,0:T(2,128)(2,1)S(1)}, u32[]{:S(2)}, u32[]{:S(2)}) async-start(bf16[512,3,2,128]{3,2,1,0:T(2,128)(2,1)} %send_pieces.1), calls=%async_computation.1 | async-start | bytes 1572864 | tf_op jit(solution)/shard_map/all_to_all | solution.py:319
  43.6 0.0 copy-done
  43.6 6.3 %collective-permute-start = (bf16[1,2,512,512]{3,2,1,0:T(8,128)(2,1)S(1)}, bf16[1,2,512,512]{3,2,1,0:T(8,128)(2,1)S(1)}, u32[]{:S(2)}, u32[]{:S(2)}) collective-permute-start(bf16[1,2,512,512]{3,2,1,0:T(8,128)(2,1)S(1)} %copy-done), channel_id=1, source_target_pairs={{0,4},{4,0},{8,12},{12,8},{16,20},{20,16},{24,28},{28,24},{32,36},... | collective-permute-start | bytes 3145736 | tf_op jit(solution)/shard_map/ppermute | solution.py:314
  50.0 0.1 pad_add_fusion.place_ref
  50.1 2.2 %collective-permute-done = bf16[1,2,512,512]{3,2,1,0:T(8,128)(2,1)S(1)} collective-permute-done((bf16[1,2,512,512]{3,2,1,0:T(8,128)(2,1)S(1)}, bf16[1,2,512,512]{3,2,1,0:T(8,128)(2,1)S(1)}, u32[]{:S(2)}, u32[]{:S(2)}) %collective-permute-start) | collective-permute-done | bytes 1048608 | tf_op jit(solution)/shard_map/ppermute | solution.py:314
  52.2 18.9 %all-to-all-done.1.funcs_ref = bf16[512,3,2,128]{3,2,1,0:T(2,128)(2,1)S(1)} async-done(((bf16[512,3,2,128]{3,2,1,0:T(2,128)(2,1)}), bf16[512,3,2,128]{3,2,1,0:T(2,128)(2,1)S(1)}, u32[]{:S(2)}, u32[]{:S(2)}) %all-to-all-start.1) | async-done | bytes 786464 | tf_op jit(solution)/shard_map/all_to_all | solution.py:319
  71.1 0.0 copy-done.1
  71.1 5.0 %pair_terms.1 = f32[128,128]{1,0:T(8,128)S(1)} custom-call(s32[2]{0:T(128)S(1)} %pad_add_fusion.place_ref, s32[8,2]{1,0:T(8,128)S(1)} %copy.11.pairs_ref, bf16[512,3,2,128]{3,2,1,0:T(2,128)(2,1)S(1)} %all-to-all-done.1.funcs_ref, bf16[2,512,512]{2,1,0:T(8,128)(2,1)S(1)} %bitcast.10, bf16[2,512,512]{2,1,0:T(8,128)(2,1)S(1)} %bitcast.11, ...), custom_call_target="tpu_custom_call" | custom-call | tf_op jit(solution)/shard_map/pair_terms/pallas_call | solution.py:289
  76.1 11.8 %all_to_all.20 = f32[16,8,128]{2,1,0:T(8,128)S(1)} all-to-all(f32[16,8,128]{2,1,0:T(8,128)S(1)} %bitcast.12), channel_id=1, replica_groups={{0,4,8,12,16,20,24,28,32,36,40,44,48,52,56,60},{64,68,72,76,80,84,88,92..., dimensions={0} | all-to-all | bytes 131072 | tf_op jit(solution)/shard_map/all_to_all | solution.py:326
  88.0 0.1 reshape.18
  88.1 12.4 %all_to_all.21 = f32[32,1,32]{2,1,0:T(1,128)S(1)} all-to-all(f32[32,1,32]{2,1,0:T(1,128)S(1)} %reshape.18), channel_id=1, replica_groups={{0,1,2,3,64,65,66,67,128,129,130,131,192,193,194,195,256,257,258,259,32..., dimensions={0} | all-to-all | bytes 8192 | tf_op jit(solution)/shard_map/all_to_all | solution.py:330
  100.4 0.1 reduce_sum.19
  100.5 0.6 reshape.19
  (1 shorter events, 0.0 us)
Async XLA Ops:
  1.6 18.6 %copy-start.2 = (s32[8,2]{0,1:T(2,128)S(1)}, s32[8,2]{0,1:T(2,128)}, u32[]{:S(2)}) copy-start(s32[8,2]{0,1:T(2,128)} %param.8) | copy-start | bytes 196
  1.6 30.8 %all-to-all-start = ((bf16[128,4,128]{2,1,0:T(4,128)(2,1)}), bf16[128,4,128]{2,1,0:T(4,128)(2,1)S(1)}, u32[]{:S(2)}, u32[]{:S(2)}) async-start(bf16[128,4,128]{2,1,0:T(4,128)(2,1)} %pack_pieces.1), calls=%async_computation | async-start | bytes 262144 | tf_op jit(solution)/shard_map/all_to_all | solution.py:317
  20.2 23.4 %copy-start = (bf16[1,2,512,512]{3,2,1,0:T(8,128)(2,1)S(1)}, bf16[1,2,512,512]{3,2,1,0:T(8,128)(2,1)}, u32[]{:S(2)}) copy-start(bf16[1,2,512,512]{3,2,1,0:T(8,128)(2,1)} %param.6) | copy-start | bytes 3145732
  34.3 36.9 %copy-start.1 = (bf16[512,256]{1,0:T(8,128)(2,1)S(1)}, bf16[512,256]{1,0:T(8,128)(2,1)}, u32[]{:S(2)}) copy-start(bf16[512,256]{1,0:T(8,128)(2,1)} %constant.13.clone.table_ref) | copy-start | bytes 786436
  34.3 36.8 %all-to-all-start.1 = ((bf16[512,3,2,128]{3,2,1,0:T(2,128)(2,1)}), bf16[512,3,2,128]{3,2,1,0:T(2,128)(2,1)S(1)}, u32[]{:S(2)}, u32[]{:S(2)}) async-start(bf16[512,3,2,128]{3,2,1,0:T(2,128)(2,1)} %send_pieces.1), calls=%async_computation.1 | async-start | bytes 1572864 | tf_op jit(solution)/shard_map/all_to_all | solution.py:319
  43.6 8.6 %collective-permute-start = (bf16[1,2,512,512]{3,2,1,0:T(8,128)(2,1)S(1)}, bf16[1,2,512,512]{3,2,1,0:T(8,128)(2,1)S(1)}, u32[]{:S(2)}, u32[]{:S(2)}) collective-permute-start(bf16[1,2,512,512]{3,2,1,0:T(8,128)(2,1)S(1)} %copy-done), channel_id=1, source_target_pairs={{0,4},{4,0},{8,12},{12,8},{16,20},{20,16},{24,28},{28,24},{32,36},... | collective-permute-start | bytes 3145736 | tf_op jit(solution)/shard_map/ppermute | solution.py:314

commit v7 on v6

--- a/solution.py
+++ b/solution.py
@@ -280,7 +280,7 @@
         total += jnp.where(k == first_point[pair], jnp.broadcast_to(direct, (points, 128)), 0.0)
     back = collect(back, gather_lo, row_lo)
     total += jnp.where(k == move, jnp.broadcast_to(back, (points, 128)), 0.0)
-    out_ref[...] = total
+    out_ref[...] = total.astype(out_ref.dtype)
 
 
 def pair_terms(place, pairs, funcs, own, other, table, held, interpret=False):
@@ -288,7 +288,7 @@
     vmem, smem = pl.BlockSpec(memory_space=pltpu.VMEM), pl.BlockSpec(memory_space=pltpu.SMEM)
     return pl.pallas_call(
         pair_body,
-        out_shape=jax.ShapeDtypeStruct((points, 128), jnp.float32),
+        out_shape=jax.ShapeDtypeStruct((points, 128), jnp.bfloat16),
         in_specs=[smem, smem] + [vmem] * 5,
         out_specs=vmem,
         scratch_shapes=[
@@ -326,7 +326,7 @@
     parts = lax.all_to_all(
         terms.reshape(16, 8, 128), "kq", 0, 0, tiled=True, axis_index_groups=rows
     )
-    parts = jnp.sum(parts, axis=0).reshape(32, 1, 32)
+    parts = jnp.sum(parts.astype(jnp.float32), axis=0).reshape(32, 1, 32)
     parts = lax.all_to_all(
         parts, ("kq", "band"), 0, 0, tiled=True, axis_index_groups=columns
     )

time: 101 us -> 101 us (level)
  no operation moved by 1% of the time
where the time goes in v7:
time: 101 us
  starting transfers between devices  34.2 us (34%)
  waiting for transfers between devices  33.2 us (33%)
  blocking collectives  23.8 us (24%)
  Pallas kernels  8.4 us (8%)
    all_to_all x1, waiting for transfers between devices, local(): lax.all_to_all(send_pieces(pair_list, held), ('kq', 'band'), 0, 0, tiled=...  18.9 us
    all_to_all x1, starting transfers between devices, local(): held = lax.all_to_all(pack_pieces(pieces, exciton), 'kq', 0, 0, tiled=True)  18.5 us
    all_to_all x1, blocking collectives, local(): lax.all_to_all(parts, ('kq', 'band'), 0, 0, tiled=True, axis_index_groups...  12.3 us
    all_to_all x1, waiting for transfers between devices, local(): held = lax.all_to_all(pack_pieces(pieces, exciton), 'kq', 0, 0, tiled=True)  12.2 us
    all_to_all x1, blocking collectives, local(): lax.all_to_all(terms.reshape(16, 8, 128), 'kq', 0, 0, tiled=True, axis_in...  11.5 us
    all_to_all x1, starting transfers between devices, local(): lax.all_to_all(send_pieces(pair_list, held), ('kq', 'band'), 0, 0, tiled=...  9.33 us
    ppermute x1, starting transfers between devices, local(): other = lax.ppermute(screening, 'kq', [(i, i ^ 1) for i in range(points)])  6.35 us
    pallas_call x1, Pallas kernels, pair_terms(): pl.pallas_call(pair_body, out_shape=jax.ShapeDtypeStruct((points, 128), j...  4.96 us
  transfers between devices with their start and end apart: 3, of which 3 were waited for; matrix products, arithmetic and copies ran while one was open for 0% of the time, Pallas kernels for 0%

profile of v7, /device:TPU:1, one launch (start us, length us, event | category | flops | bytes accessed | tf_op | source)
XLA Modules:
  0.0 100.7 jit_solution(1364164037578136741)
XLA Ops:
  0.0 1.6 %pack_pieces.1 = bf16[128,4,128]{2,1,0:T(4,128)(2,1)} custom-call(bf16[128,2,128]{2,1,0:T(2,128)(2,1)} %bitcast.13, bf16[1,2,64]{2,1,0:T(2,128)(2,1)} %exciton_ref.1), custom_call_target="tpu_custom_call" | custom-call | tf_op jit(solution)/shard_map/pack_pieces/pallas_call | solution.py:64
  1.6 0.0 copy-start.2
  1.6 18.5 %all-to-all-start = ((bf16[128,4,128]{2,1,0:T(4,128)(2,1)}), bf16[128,4,128]{2,1,0:T(4,128)(2,1)S(1)}, u32[]{:S(2)}, u32[]{:S(2)}) async-start(bf16[128,4,128]{2,1,0:T(4,128)(2,1)} %pack_pieces.1), calls=%async_computation | async-start | bytes 262144 | tf_op jit(solution)/shard_map/all_to_all | solution.py:317
  20.1 0.0 copy-done.2
  20.1 0.1 copy.11.pairs_ref
  20.2 0.0 copy-start
  20.2 12.2 %all-to-all-done.held_ref = bf16[128,4,128]{2,1,0:T(4,128)(2,1)S(1)} async-done(((bf16[128,4,128]{2,1,0:T(4,128)(2,1)}), bf16[128,4,128]{2,1,0:T(4,128)(2,1)S(1)}, u32[]{:S(2)}, u32[]{:S(2)}) %all-to-all-start) | async-done | bytes 131104 | tf_op jit(solution)/shard_map/all_to_all | solution.py:317
  32.4 1.9 %send_pieces.1 = bf16[512,3,2,128]{3,2,1,0:T(2,128)(2,1)} custom-call(s32[8,2]{1,0:T(8,128)S(1)} %copy.11.pairs_ref, bf16[128,4,128]{2,1,0:T(4,128)(2,1)S(1)} %all-to-all-done.held_ref), custom_call_target="tpu_custom_call" | custom-call | tf_op jit(solution)/shard_map/send_pieces/pallas_call | solution.py:106
  34.3 0.0 copy-start.1
  34.3 9.3 %all-to-all-start.1 = ((bf16[512,3,2,128]{3,2,1,0:T(2,128)(2,1)}), bf16[512,3,2,128]{3,2,1,0:T(2,128)(2,1)S(1)}, u32[]{:S(2)}, u32[]{:S(2)}) async-start(bf16[512,3,2,128]{3,2,1,0:T(2,128)(2,1)} %send_pieces.1), calls=%async_computation.1 | async-start | bytes 1572864 | tf_op jit(solution)/shard_map/all_to_all | solution.py:319
  43.6 0.0 copy-done
  43.6 6.3 %collective-permute-start = (bf16[1,2,512,512]{3,2,1,0:T(8,128)(2,1)S(1)}, bf16[1,2,512,512]{3,2,1,0:T(8,128)(2,1)S(1)}, u32[]{:S(2)}, u32[]{:S(2)}) collective-permute-start(bf16[1,2,512,512]{3,2,1,0:T(8,128)(2,1)S(1)} %copy-done), channel_id=1, source_target_pairs={{0,4},{4,0},{8,12},{12,8},{16,20},{20,16},{24,28},{28,24},{32,36},... | collective-permute-start | bytes 3145736 | tf_op jit(solution)/shard_map/ppermute | solution.py:314
  50.0 0.1 pad_add_fusion.place_ref
  50.1 2.2 %collective-permute-done = bf16[1,2,512,512]{3,2,1,0:T(8,128)(2,1)S(1)} collective-permute-done((bf16[1,2,512,512]{3,2,1,0:T(8,128)(2,1)S(1)}, bf16[1,2,512,512]{3,2,1,0:T(8,128)(2,1)S(1)}, u32[]{:S(2)}, u32[]{:S(2)}) %collective-permute-start) | collective-permute-done | bytes 1048608 | tf_op jit(solution)/shard_map/ppermute | solution.py:314
  52.2 18.9 %all-to-all-done.1.funcs_ref = bf16[512,3,2,128]{3,2,1,0:T(2,128)(2,1)S(1)} async-done(((bf16[512,3,2,128]{3,2,1,0:T(2,128)(2,1)}), bf16[512,3,2,128]{3,2,1,0:T(2,128)(2,1)S(1)}, u32[]{:S(2)}, u32[]{:S(2)}) %all-to-all-start.1) | async-done | bytes 786464 | tf_op jit(solution)/shard_map/all_to_all | solution.py:319
  71.1 0.0 copy-done.1
  71.1 5.0 %pair_terms.1 = bf16[128,128]{1,0:T(8,128)(2,1)S(1)} custom-call(s32[2]{0:T(128)S(1)} %pad_add_fusion.place_ref, s32[8,2]{1,0:T(8,128)S(1)} %copy.11.pairs_ref, bf16[512,3,2,128]{3,2,1,0:T(2,128)(2,1)S(1)} %all-to-all-done.1.funcs_ref, bf16[2,512,512]{2,1,0:T(8,128)(2,1)S(1)} %bitcast.10, bf16[2,512,512]{2,1,0:T(8,128)(2,1)S(1)} %bitcast.11, ...), custom_call_target="tpu_custom_call" | custom-call | tf_op jit(solution)/shard_map/pair_terms/pallas_call | solution.py:289
  76.1 11.5 %all_to_all.20 = bf16[16,8,128]{2,1,0:T(8,128)(2,1)S(1)} all-to-all(bf16[16,8,128]{2,1,0:T(8,128)(2,1)S(1)} %bitcast.12), channel_id=1, replica_groups={{0,4,8,12,16,20,24,28,32,36,40,44,48,52,56,60},{64,68,72,76,80,84,88,92..., dimensions={0} | all-to-all | bytes 65536 | tf_op jit(solution)/shard_map/all_to_all | solution.py:326
  87.6 0.1 reshape.18
  87.7 12.3 %all_to_all.21 = f32[32,1,32]{2,1,0:T(1,128)S(1)} all-to-all(f32[32,1,32]{2,1,0:T(1,128)S(1)} %reshape.18), channel_id=1, replica_groups={{0,1,2,3,64,65,66,67,128,129,130,131,192,193,194,195,256,257,258,259,32..., dimensions={0} | all-to-all | bytes 8192 | tf_op jit(solution)/shard_map/all_to_all | solution.py:330
  100.0 0.1 reduce_sum.19
  100.0 0.6 reshape.19
  (1 shorter events, 0.0 us)
Async XLA Ops:
  1.6 18.6 %copy-start.2 = (s32[8,2]{0,1:T(2,128)S(1)}, s32[8,2]{0,1:T(2,128)}, u32[]{:S(2)}) copy-start(s32[8,2]{0,1:T(2,128)} %param.8) | copy-start | bytes 196
  1.6 30.8 %all-to-all-start = ((bf16[128,4,128]{2,1,0:T(4,128)(2,1)}), bf16[128,4,128]{2,1,0:T(4,128)(2,1)S(1)}, u32[]{:S(2)}, u32[]{:S(2)}) async-start(bf16[128,4,128]{2,1,0:T(4,128)(2,1)} %pack_pieces.1), calls=%async_computation | async-start | bytes 262144 | tf_op jit(solution)/shard_map/all_to_all | solution.py:317
  20.2 23.4 %copy-start = (bf16[1,2,512,512]{3,2,1,0:T(8,128)(2,1)S(1)}, bf16[1,2,512,512]{3,2,1,0:T(8,128)(2,1)}, u32[]{:S(2)}) copy-start(bf16[1,2,512,512]{3,2,1,0:T(8,128)(2,1)} %param.6) | copy-start | bytes 3145732
  34.3 36.9 %copy-start.1 = (bf16[512,256]{1,0:T(8,128)(2,1)S(1)}, bf16[512,256]{1,0:T(8,128)(2,1)}, u32[]{:S(2)}) copy-start(bf16[512,256]{1,0:T(8,128)(2,1)} %constant.13.clone.table_ref) | copy-start | bytes 786436
  34.3 36.8 %all-to-all-start.1 = ((bf16[512,3,2,128]{3,2,1,0:T(2,128)(2,1)}), bf16[512,3,2,128]{3,2,1,0:T(2,128)(2,1)S(1)}, u32[]{:S(2)}, u32[]{:S(2)}) async-start(bf16[512,3,2,128]{3,2,1,0:T(2,128)(2,1)} %send_pieces.1), calls=%async_computation.1 | async-start | bytes 1572864 | tf_op jit(solution)/shard_map/all_to_all | solution.py:319
  43.6 8.6 %collective-permute-start = (bf16[1,2,512,512]{3,2,1,0:T(8,128)(2,1)S(1)}, bf16[1,2,512,512]{3,2,1,0:T(8,128)(2,1)S(1)}, u32[]{:S(2)}, u32[]{:S(2)}) collective-permute-start(bf16[1,2,512,512]{3,2,1,0:T(8,128)(2,1)S(1)} %copy-done), channel_id=1, source_target_pairs={{0,4},{4,0},{8,12},{12,8},{16,20},{20,16},{24,28},{28,24},{32,36},... | collective-permute-start | bytes 3145736 | tf_op jit(solution)/shard_map/ppermute | solution.py:314

commit v8 on v6

--- a/solution.py
+++ b/solution.py
@@ -261,8 +261,7 @@
         both = sum(jnp.dot(p, gather, preferred_element_type=f32) for p in (high, middle, low))
         return jnp.sum(jnp.where(row_band == (lane & 7), both, 0.0), axis=0, keepdims=True)
 
-    r = iota((points, 128), 0)
-    k = ((r & 7) << 4) | (r >> 3)
+    k = iota((points, 128), 0)
     total = jnp.zeros((points, 128), f32)
     back = 0.0
     for pair, weights in enumerate((own_ref, other_ref)):
@@ -321,15 +320,9 @@
     table = jnp.asarray(plane_table(), dtype=bf16)
     terms = pair_terms(place, pair_list, funcs, screening[0], other[0], table, held)
 
-    rows = [[16 * y + z for z in range(16)] for y in range(8)]
-    columns = [[(16 * y + z) * BLOCKS + b for y in range(8) for b in range(BLOCKS)] for z in range(16)]
-    parts = lax.all_to_all(
-        terms.reshape(16, 8, 128), "kq", 0, 0, tiled=True, axis_index_groups=rows
-    )
-    parts = jnp.sum(parts, axis=0).reshape(32, 1, 32)
-    parts = lax.all_to_all(
-        parts, ("kq", "band"), 0, 0, tiled=True, axis_index_groups=columns
-    )
+    parts = lax.all_to_all(terms.reshape(points, 1, 128), "kq", 0, 0, tiled=True)
+    parts = jnp.sum(parts, axis=0).reshape(BLOCKS, 1, 32)
+    parts = lax.all_to_all(parts, "band", 0, 0, tiled=True)
     return jnp.sum(parts, axis=(0, 1)).reshape(1, 2, 16)
 
 

time: 101 us -> 102 us (level)
  no operation moved by 1% of the time
where the time goes in v8:
time: 102 us
  starting transfers between devices  34.2 us (34%)
  waiting for transfers between devices  33.2 us (33%)
  blocking collectives  24.9 us (24%)
  Pallas kernels  8.38 us (8%)
    all_to_all x1, waiting for transfers between devices, local(): lax.all_to_all(send_pieces(pair_list, held), ('kq', 'band'), 0, 0, tiled=...  18.9 us
    all_to_all x1, starting transfers between devices, local(): held = lax.all_to_all(pack_pieces(pieces, exciton), 'kq', 0, 0, tiled=True)  18.5 us
    all_to_all x1, blocking collectives, local(): lax.all_to_all(terms.reshape(points, 1, 128), 'kq', 0, 0, tiled=True)  18.4 us
    all_to_all x1, waiting for transfers between devices, local(): held = lax.all_to_all(pack_pieces(pieces, exciton), 'kq', 0, 0, tiled=True)  12.2 us
    all_to_all x1, starting transfers between devices, local(): lax.all_to_all(send_pieces(pair_list, held), ('kq', 'band'), 0, 0, tiled=...  9.33 us
    all_to_all x1, blocking collectives, local(): parts = lax.all_to_all(parts, 'band', 0, 0, tiled=True)  6.46 us
    ppermute x1, starting transfers between devices, local(): other = lax.ppermute(screening, 'kq', [(i, i ^ 1) for i in range(points)])  6.35 us
    pallas_call x1, Pallas kernels, pair_terms(): pl.pallas_call(pair_body, out_shape=jax.ShapeDtypeStruct((points, 128), j...  4.94 us
  transfers between devices with their start and end apart: 3, of which 3 were waited for; matrix products, arithmetic and copies ran while one was open for 0% of the time, Pallas kernels for 0%

profile of v8, /device:TPU:1, one launch (start us, length us, event | category | flops | bytes accessed | tf_op | source)
XLA Modules:
  0.0 101.9 jit_solution(6340692049719506206)
XLA Ops:
  0.0 1.6 %pack_pieces.1 = bf16[128,4,128]{2,1,0:T(4,128)(2,1)} custom-call(bf16[128,2,128]{2,1,0:T(2,128)(2,1)} %bitcast.16, bf16[1,2,64]{2,1,0:T(2,128)(2,1)} %exciton_ref.1), custom_call_target="tpu_custom_call" | custom-call | tf_op jit(solution)/shard_map/pack_pieces/pallas_call | solution.py:64
  1.6 0.0 copy-start.2
  1.6 18.5 %all-to-all-start = ((bf16[128,4,128]{2,1,0:T(4,128)(2,1)}), bf16[128,4,128]{2,1,0:T(4,128)(2,1)S(1)}, u32[]{:S(2)}, u32[]{:S(2)}) async-start(bf16[128,4,128]{2,1,0:T(4,128)(2,1)} %pack_pieces.1), calls=%async_computation | async-start | bytes 262144 | tf_op jit(solution)/shard_map/all_to_all | solution.py:316
  20.1 0.0 copy-done.2
  20.1 0.1 copy.11.pairs_ref
  20.2 0.0 copy-start
  20.2 12.2 %all-to-all-done.held_ref = bf16[128,4,128]{2,1,0:T(4,128)(2,1)S(1)} async-done(((bf16[128,4,128]{2,1,0:T(4,128)(2,1)}), bf16[128,4,128]{2,1,0:T(4,128)(2,1)S(1)}, u32[]{:S(2)}, u32[]{:S(2)}) %all-to-all-start) | async-done | bytes 131104 | tf_op jit(solution)/shard_map/all_to_all | solution.py:316
  32.4 1.9 %send_pieces.1 = bf16[512,3,2,128]{3,2,1,0:T(2,128)(2,1)} custom-call(s32[8,2]{1,0:T(8,128)S(1)} %copy.11.pairs_ref, bf16[128,4,128]{2,1,0:T(4,128)(2,1)S(1)} %all-to-all-done.held_ref), custom_call_target="tpu_custom_call" | custom-call | tf_op jit(solution)/shard_map/send_pieces/pallas_call | solution.py:106
  34.3 0.0 copy-start.1
  34.3 9.3 %all-to-all-start.1 = ((bf16[512,3,2,128]{3,2,1,0:T(2,128)(2,1)}), bf16[512,3,2,128]{3,2,1,0:T(2,128)(2,1)S(1)}, u32[]{:S(2)}, u32[]{:S(2)}) async-start(bf16[512,3,2,128]{3,2,1,0:T(2,128)(2,1)} %send_pieces.1), calls=%async_computation.1 | async-start | bytes 1572864 | tf_op jit(solution)/shard_map/all_to_all | solution.py:318
  43.6 0.0 copy-done
  43.6 6.3 %collective-permute-start = (bf16[1,2,512,512]{3,2,1,0:T(8,128)(2,1)S(1)}, bf16[1,2,512,512]{3,2,1,0:T(8,128)(2,1)S(1)}, u32[]{:S(2)}, u32[]{:S(2)}) collective-permute-start(bf16[1,2,512,512]{3,2,1,0:T(8,128)(2,1)S(1)} %copy-done), channel_id=1, source_target_pairs={{0,4},{4,0},{8,12},{12,8},{16,20},{20,16},{24,28},{28,24},{32,36},... | collective-permute-start | bytes 3145736 | tf_op jit(solution)/shard_map/ppermute | solution.py:313
  50.0 0.1 pad_add_fusion.place_ref
  50.1 2.2 %collective-permute-done = bf16[1,2,512,512]{3,2,1,0:T(8,128)(2,1)S(1)} collective-permute-done((bf16[1,2,512,512]{3,2,1,0:T(8,128)(2,1)S(1)}, bf16[1,2,512,512]{3,2,1,0:T(8,128)(2,1)S(1)}, u32[]{:S(2)}, u32[]{:S(2)}) %collective-permute-start) | collective-permute-done | bytes 1048608 | tf_op jit(solution)/shard_map/ppermute | solution.py:313
  52.2 18.9 %all-to-all-done.1.funcs_ref = bf16[512,3,2,128]{3,2,1,0:T(2,128)(2,1)S(1)} async-done(((bf16[512,3,2,128]{3,2,1,0:T(2,128)(2,1)}), bf16[512,3,2,128]{3,2,1,0:T(2,128)(2,1)S(1)}, u32[]{:S(2)}, u32[]{:S(2)}) %all-to-all-start.1) | async-done | bytes 786464 | tf_op jit(solution)/shard_map/all_to_all | solution.py:318
  71.1 0.0 copy-done.1
  71.1 4.9 %pair_terms.1 = f32[128,128]{1,0:T(8,128)S(1)} custom-call(s32[2]{0:T(128)S(1)} %pad_add_fusion.place_ref, s32[8,2]{1,0:T(8,128)S(1)} %copy.11.pairs_ref, bf16[512,3,2,128]{3,2,1,0:T(2,128)(2,1)S(1)} %all-to-all-done.1.funcs_ref, bf16[2,512,512]{2,1,0:T(8,128)(2,1)S(1)} %bitcast.13, bf16[2,512,512]{2,1,0:T(8,128)(2,1)S(1)} %bitcast.14, ...), custom_call_target="tpu_custom_call" | custom-call | tf_op jit(solution)/shard_map/pair_terms/pallas_call | solution.py:288
  76.1 18.4 %all_to_all.20 = f32[128,1,128]{2,1,0:T(1,128)S(1)} all-to-all(f32[128,1,128]{2,1,0:T(1,128)S(1)} %bitcast.15), channel_id=1, replica_groups=mesh['kq'=128,'band'=4] {'kq'}, dimensions={0} | all-to-all | bytes 131072 | tf_op jit(solution)/shard_map/all_to_all | solution.py:323
  94.5 0.2 reduce_sum.18
  94.7 0.1 reshape.20
  94.8 6.5 %all_to_all.21 = f32[4,1,32]{2,1,0:T(1,128)S(1)} all-to-all(f32[4,1,32]{2,1,0:T(1,128)S(1)} %bitcast.17), channel_id=1, replica_groups=mesh['kq'=128,'band'=4] {'band'}, dimensions={0} | all-to-all | bytes 1024 | tf_op jit(solution)/shard_map/all_to_all | solution.py:325
  101.2 0.6 reshape.21
  (1 shorter events, 0.0 us)
Async XLA Ops:
  1.6 18.6 %copy-start.2 = (s32[8,2]{0,1:T(2,128)S(1)}, s32[8,2]{0,1:T(2,128)}, u32[]{:S(2)}) copy-start(s32[8,2]{0,1:T(2,128)} %param.8) | copy-start | bytes 196
  1.6 30.8 %all-to-all-start = ((bf16[128,4,128]{2,1,0:T(4,128)(2,1)}), bf16[128,4,128]{2,1,0:T(4,128)(2,1)S(1)}, u32[]{:S(2)}, u32[]{:S(2)}) async-start(bf16[128,4,128]{2,1,0:T(4,128)(2,1)} %pack_pieces.1), calls=%async_computation | async-start | bytes 262144 | tf_op jit(solution)/shard_map/all_to_all | solution.py:316
  20.2 23.4 %copy-start = (bf16[1,2,512,512]{3,2,1,0:T(8,128)(2,1)S(1)}, bf16[1,2,512,512]{3,2,1,0:T(8,128)(2,1)}, u32[]{:S(2)}) copy-start(bf16[1,2,512,512]{3,2,1,0:T(8,128)(2,1)} %param.6) | copy-start | bytes 3145732
  34.3 36.9 %copy-start.1 = (bf16[512,256]{1,0:T(8,128)(2,1)S(1)}, bf16[512,256]{1,0:T(8,128)(2,1)}, u32[]{:S(2)}) copy-start(bf16[512,256]{1,0:T(8,128)(2,1)} %constant.13.clone.table_ref) | copy-start | bytes 786436
  34.3 36.8 %all-to-all-start.1 = ((bf16[512,3,2,128]{3,2,1,0:T(2,128)(2,1)}), bf16[512,3,2,128]{3,2,1,0:T(2,128)(2,1)S(1)}, u32[]{:S(2)}, u32[]{:S(2)}) async-start(bf16[512,3,2,128]{3,2,1,0:T(2,128)(2,1)} %send_pieces.1), calls=%async_computation.1 | async-start | bytes 1572864 | tf_op jit(solution)/shard_map/all_to_all | solution.py:318
  43.6 8.6 %collective-permute-start = (bf16[1,2,512,512]{3,2,1,0:T(8,128)(2,1)S(1)}, bf16[1,2,512,512]{3,2,1,0:T(8,128)(2,1)S(1)}, u32[]{:S(2)}, u32[]{:S(2)}) collective-permute-start(bf16[1,2,512,512]{3,2,1,0:T(8,128)(2,1)S(1)} %copy-done), channel_id=1, source_target_pairs={{0,4},{4,0},{8,12},{12,8},{16,20},{20,16},{24,28},{28,24},{32,36},... | collective-permute-start | bytes 3145736 | tf_op jit(solution)/shard_map/ppermute | solution.py:313

commit v9 on v7

--- a/solution.py
+++ b/solution.py
@@ -51,21 +51,40 @@
     return seconds_ref[2 * block + parity, 1]
 
 
-def pack_body(pieces_ref, exciton_ref, packed_ref):
-    points = pieces_ref.shape[0]
+def pack_body(pieces_ref, exciton_ref, packed_ref, arrived, built, came, went):
+    half = built.shape[0] // 2
+    rows = [pl.ds(0, half), pl.ds(half, half)]
+    incoming = [
+        pltpu.make_async_copy(pieces_ref.at[rows[h]], arrived.at[rows[h]], came.at[h]) for h in range(2)
+    ]
+    outgoing = [
+        pltpu.make_async_copy(built.at[rows[h]], packed_ref.at[rows[h]], went.at[h]) for h in range(2)
+    ]
+    for copy in incoming:
+        copy.start()
     amps = jnp.concatenate([exciton_ref[0], jnp.zeros((2, 64), jnp.bfloat16)], axis=1)
-    packed_ref[:, 0:2] = pieces_ref[...]
-    packed_ref[:, 2:4] = jnp.broadcast_to(amps[None], (points, 2, 128))
+    for h in range(2):
+        built[rows[h], 2:4] = jnp.broadcast_to(amps[None], (half, 2, 128))
+        incoming[h].wait()
+        built[rows[h], 0:2] = arrived[rows[h]]
+        outgoing[h].start()
+    for copy in outgoing:
+        copy.wait()
 
 
 def pack_pieces(pieces, exciton, interpret=False):
     points = pieces.shape[0]
-    vmem = pl.BlockSpec(memory_space=pltpu.VMEM)
     return pl.pallas_call(
         pack_body,
         out_shape=jax.ShapeDtypeStruct((points, 4, 128), jnp.bfloat16),
-        in_specs=[vmem, vmem],
-        out_specs=vmem,
+        in_specs=[pl.BlockSpec(memory_space=pl.ANY), pl.BlockSpec(memory_space=pltpu.VMEM)],
+        out_specs=pl.BlockSpec(memory_space=pl.ANY),
+        scratch_shapes=[
+            pltpu.VMEM((points, 2, 128), jnp.bfloat16),
+            pltpu.VMEM((points, 4, 128), jnp.bfloat16),
+            pltpu.SemaphoreType.DMA((2,)),
+            pltpu.SemaphoreType.DMA((2,)),
+        ],
         name="pack_pieces",
         interpret=interpret,
     )(pieces, exciton)

time: 101 us -> 102 us (level)
  no operation moved by 1% of the time
where the time goes in v9:
time: 102 us; the launch traced here: 101 us
  starting transfers between devices  34.1 us (33%)
  waiting for transfers between devices  33.2 us (33%)
  blocking collectives  23.8 us (23%)
  Pallas kernels  8.98 us (9%)
    all_to_all x1, waiting for transfers between devices, local(): lax.all_to_all(send_pieces(pair_list, held), ('kq', 'band'), 0, 0, tiled=...  18.9 us
    all_to_all x1, starting transfers between devices, local(): held = lax.all_to_all(pack_pieces(pieces, exciton), 'kq', 0, 0, tiled=True)  18.4 us
    all_to_all x1, blocking collectives, local(): lax.all_to_all(parts, ('kq', 'band'), 0, 0, tiled=True, axis_index_groups...  12.3 us
    all_to_all x1, waiting for transfers between devices, local(): held = lax.all_to_all(pack_pieces(pieces, exciton), 'kq', 0, 0, tiled=True)  12.2 us
    all_to_all x1, blocking collectives, local(): lax.all_to_all(terms.reshape(16, 8, 128), 'kq', 0, 0, tiled=True, axis_in...  11.5 us
    all_to_all x1, starting transfers between devices, local(): lax.all_to_all(send_pieces(pair_list, held), ('kq', 'band'), 0, 0, tiled=...  9.33 us
    ppermute x1, starting transfers between devices, local(): other = lax.ppermute(screening, 'kq', [(i, i ^ 1) for i in range(points)])  6.35 us
    pallas_call x1, Pallas kernels, pair_terms(): pl.pallas_call(pair_body, out_shape=jax.ShapeDtypeStruct((points, 128), j...  4.97 us
  transfers between devices with their start and end apart: 3, of which 3 were waited for; matrix products, arithmetic and copies ran while one was open for 0% of the time, Pallas kernels for 0%

profile of v9, /device:TPU:1, one launch (start us, length us, event | category | flops | bytes accessed | tf_op | source)
XLA Modules:
  0.0 101.2 jit_solution(17166585499285690002)
XLA Ops:
  0.0 2.1 %pack_pieces.1 = bf16[128,4,128]{2,1,0:T(4,128)(2,1)} custom-call(bf16[128,2,128]{2,1,0:T(2,128)(2,1)} %bitcast.13, bf16[1,2,64]{2,1,0:T(2,128)(2,1)} %exciton_ref.1), custom_call_target="tpu_custom_call" | custom-call | tf_op jit(solution)/shard_map/pack_pieces/pallas_call | solution.py:77
  2.1 0.0 copy-start.2
  2.2 18.4 %all-to-all-start = ((bf16[128,4,128]{2,1,0:T(4,128)(2,1)}), bf16[128,4,128]{2,1,0:T(4,128)(2,1)S(1)}, u32[]{:S(2)}, u32[]{:S(2)}) async-start(bf16[128,4,128]{2,1,0:T(4,128)(2,1)} %pack_pieces.1), calls=%async_computation | async-start | bytes 262144 | tf_op jit(solution)/shard_map/all_to_all | solution.py:336
  20.6 0.0 copy-done.2
  20.6 0.1 copy.11.pairs_ref
  20.7 0.0 copy-start
  20.7 12.2 %all-to-all-done.held_ref = bf16[128,4,128]{2,1,0:T(4,128)(2,1)S(1)} async-done(((bf16[128,4,128]{2,1,0:T(4,128)(2,1)}), bf16[128,4,128]{2,1,0:T(4,128)(2,1)S(1)}, u32[]{:S(2)}, u32[]{:S(2)}) %all-to-all-start) | async-done | bytes 131104 | tf_op jit(solution)/shard_map/all_to_all | solution.py:336
  32.8 1.9 %send_pieces.1 = bf16[512,3,2,128]{3,2,1,0:T(2,128)(2,1)} custom-call(s32[8,2]{1,0:T(8,128)S(1)} %copy.11.pairs_ref, bf16[128,4,128]{2,1,0:T(4,128)(2,1)S(1)} %all-to-all-done.held_ref), custom_call_target="tpu_custom_call" | custom-call | tf_op jit(solution)/shard_map/send_pieces/pallas_call | solution.py:125
  34.7 0.0 copy-start.1
  34.7 9.3 %all-to-all-start.1 = ((bf16[512,3,2,128]{3,2,1,0:T(2,128)(2,1)}), bf16[512,3,2,128]{3,2,1,0:T(2,128)(2,1)S(1)}, u32[]{:S(2)}, u32[]{:S(2)}) async-start(bf16[512,3,2,128]{3,2,1,0:T(2,128)(2,1)} %send_pieces.1), calls=%async_computation.1 | async-start | bytes 1572864 | tf_op jit(solution)/shard_map/all_to_all | solution.py:338
  44.1 0.0 copy-done
  44.1 6.3 %collective-permute-start = (bf16[1,2,512,512]{3,2,1,0:T(8,128)(2,1)S(1)}, bf16[1,2,512,512]{3,2,1,0:T(8,128)(2,1)S(1)}, u32[]{:S(2)}, u32[]{:S(2)}) collective-permute-start(bf16[1,2,512,512]{3,2,1,0:T(8,128)(2,1)S(1)} %copy-done), channel_id=1, source_target_pairs={{0,4},{4,0},{8,12},{12,8},{16,20},{20,16},{24,28},{28,24},{32,36},... | collective-permute-start | bytes 3145736 | tf_op jit(solution)/shard_map/ppermute | solution.py:333
  50.5 0.1 pad_add_fusion.place_ref
  50.5 2.2 %collective-permute-done = bf16[1,2,512,512]{3,2,1,0:T(8,128)(2,1)S(1)} collective-permute-done((bf16[1,2,512,512]{3,2,1,0:T(8,128)(2,1)S(1)}, bf16[1,2,512,512]{3,2,1,0:T(8,128)(2,1)S(1)}, u32[]{:S(2)}, u32[]{:S(2)}) %collective-permute-start) | collective-permute-done | bytes 1048608 | tf_op jit(solution)/shard_map/ppermute | solution.py:333
  52.7 18.9 %all-to-all-done.1.funcs_ref = bf16[512,3,2,128]{3,2,1,0:T(2,128)(2,1)S(1)} async-done(((bf16[512,3,2,128]{3,2,1,0:T(2,128)(2,1)}), bf16[512,3,2,128]{3,2,1,0:T(2,128)(2,1)S(1)}, u32[]{:S(2)}, u32[]{:S(2)}) %all-to-all-start.1) | async-done | bytes 786464 | tf_op jit(solution)/shard_map/all_to_all | solution.py:338
  71.6 0.0 copy-done.1
  71.6 5.0 %pair_terms.1 = bf16[128,128]{1,0:T(8,128)(2,1)S(1)} custom-call(s32[2]{0:T(128)S(1)} %pad_add_fusion.place_ref, s32[8,2]{1,0:T(8,128)S(1)} %copy.11.pairs_ref, bf16[512,3,2,128]{3,2,1,0:T(2,128)(2,1)S(1)} %all-to-all-done.1.funcs_ref, bf16[2,512,512]{2,1,0:T(8,128)(2,1)S(1)} %bitcast.10, bf16[2,512,512]{2,1,0:T(8,128)(2,1)S(1)} %bitcast.11, ...), custom_call_target="tpu_custom_call" | custom-call | tf_op jit(solution)/shard_map/pair_terms/pallas_call | solution.py:308
  76.6 11.5 %all_to_all.20 = bf16[16,8,128]{2,1,0:T(8,128)(2,1)S(1)} all-to-all(bf16[16,8,128]{2,1,0:T(8,128)(2,1)S(1)} %bitcast.12), channel_id=1, replica_groups={{0,4,8,12,16,20,24,28,32,36,40,44,48,52,56,60},{64,68,72,76,80,84,88,92..., dimensions={0} | all-to-all | bytes 65536 | tf_op jit(solution)/shard_map/all_to_all | solution.py:345
  88.1 0.1 reshape.18
  88.1 12.3 %all_to_all.21 = f32[32,1,32]{2,1,0:T(1,128)S(1)} all-to-all(f32[32,1,32]{2,1,0:T(1,128)S(1)} %reshape.18), channel_id=1, replica_groups={{0,1,2,3,64,65,66,67,128,129,130,131,192,193,194,195,256,257,258,259,32..., dimensions={0} | all-to-all | bytes 8192 | tf_op jit(solution)/shard_map/all_to_all | solution.py:349
  100.5 0.1 reduce_sum.19
  100.5 0.6 reshape.19
  (1 shorter events, 0.0 us)
Async XLA Ops:
  2.1 18.4 %copy-start.2 = (s32[8,2]{0,1:T(2,128)S(1)}, s32[8,2]{0,1:T(2,128)}, u32[]{:S(2)}) copy-start(s32[8,2]{0,1:T(2,128)} %param.8) | copy-start | bytes 196
  2.2 30.7 %all-to-all-start = ((bf16[128,4,128]{2,1,0:T(4,128)(2,1)}), bf16[128,4,128]{2,1,0:T(4,128)(2,1)S(1)}, u32[]{:S(2)}, u32[]{:S(2)}) async-start(bf16[128,4,128]{2,1,0:T(4,128)(2,1)} %pack_pieces.1), calls=%async_computation | async-start | bytes 262144 | tf_op jit(solution)/shard_map/all_to_all | solution.py:336
  20.7 23.4 %copy-start = (bf16[1,2,512,512]{3,2,1,0:T(8,128)(2,1)S(1)}, bf16[1,2,512,512]{3,2,1,0:T(8,128)(2,1)}, u32[]{:S(2)}) copy-start(bf16[1,2,512,512]{3,2,1,0:T(8,128)(2,1)} %param.6) | copy-start | bytes 3145732
  34.7 36.9 %copy-start.1 = (bf16[512,256]{1,0:T(8,128)(2,1)S(1)}, bf16[512,256]{1,0:T(8,128)(2,1)}, u32[]{:S(2)}) copy-start(bf16[512,256]{1,0:T(8,128)(2,1)} %constant.13.clone.table_ref) | copy-start | bytes 786436
  34.7 36.8 %all-to-all-start.1 = ((bf16[512,3,2,128]{3,2,1,0:T(2,128)(2,1)}), bf16[512,3,2,128]{3,2,1,0:T(2,128)(2,1)S(1)}, u32[]{:S(2)}, u32[]{:S(2)}) async-start(bf16[512,3,2,128]{3,2,1,0:T(2,128)(2,1)} %send_pieces.1), calls=%async_computation.1 | async-start | bytes 1572864 | tf_op jit(solution)/shard_map/all_to_all | solution.py:338
  44.1 8.6 %collective-permute-start = (bf16[1,2,512,512]{3,2,1,0:T(8,128)(2,1)S(1)}, bf16[1,2,512,512]{3,2,1,0:T(8,128)(2,1)S(1)}, u32[]{:S(2)}, u32[]{:S(2)}) collective-permute-start(bf16[1,2,512,512]{3,2,1,0:T(8,128)(2,1)S(1)} %copy-done), channel_id=1, source_target_pairs={{0,4},{4,0},{8,12},{12,8},{16,20},{20,16},{24,28},{28,24},{32,36},... | collective-permute-start | bytes 3145736 | tf_op jit(solution)/shard_map/ppermute | solution.py:333
